TPU v7x, 32 devices: a whole 2x2x4 slice. The times are simulated.
32 devices in a mesh: ra: 4 (over x, core), rb: 8 (over z, y).
Axes of the slice: x: 2, y: 2, z: 4, core: 2. Of those that a mesh axis runs over, the one named last changes fastest.
Arguments:
- amplitude: bfloat16 [2, 512, 512, 256], P(None, 'ra', 'rb'), may hold values from -6 to 6
- coupling: bfloat16 [6, 256, 256], replicated, may hold values from -0.5 to 0.5
- pattern: int32 [6, 4, 4], replicated, may hold values 0 or 1
- radial: float32 [6, 512, 512], P(None, 'ra', 'rb'), may hold values from -2.4 to 2.4
- first_prop: bfloat16 [2, 512, 512], replicated, may hold values from -0.1875 to 0.1875
- second_prop: bfloat16 [2, 512, 512], replicated, may hold values from -0.1875 to 0.1875
Outputs:
- evolved: bfloat16 [2, 512, 512, 256], P(None, 'ra', 'rb')
All inputs are finite; a program needn't handle non-finite values.
Results may differ from a plain program's by a relative error of at most 0.0095.
Values may be sent and summed in bfloat16 or wider, within the bound.
A program may use at most 128 MiB of HBM per device.

v0:
```python
import functools

import jax
import jax.numpy as jnp
from jax import lax
from jax.experimental import pallas as pl
from jax.experimental.pallas import tpu as pltpu
from jax.sharding import PartitionSpec as P


KTERMS = 6
STEPS = 2
LANES = 128
TILE = 16


def complex_rows(matrix, piece):
    form = "ac,cqw->aqw"
    real_part = jnp.einsum(
        form, matrix[0], piece[0], preferred_element_type=jnp.float32
    ) - jnp.einsum(form, matrix[1], piece[1], preferred_element_type=jnp.float32)
    imag_part = jnp.einsum(
        form, matrix[0], piece[1], preferred_element_type=jnp.float32
    ) + jnp.einsum(form, matrix[1], piece[0], preferred_element_type=jnp.float32)
    return jnp.stack([real_part, imag_part]).astype(jnp.bfloat16)


def masked_weights(coupling, pattern):
    channels = coupling.shape[1]
    count = pattern.shape[1]
    block_size = channels // count
    spread = jnp.broadcast_to(
        pattern[:, :, None, :, None], (KTERMS, count, block_size, count, block_size)
    )
    return coupling * spread.reshape(KTERMS, channels, channels).astype(jnp.bfloat16)


def plain(amplitude, coupling, pattern, radial, first_prop, second_prop):
    first_rows, second_rows, channels = (amplitude.shape[1], amplitude.shape[2], amplitude.shape[3])
    cells = first_rows * second_rows
    groups_a = lax.axis_size("ra")
    groups_b = lax.axis_size("rb")
    width_a = channels // groups_a
    width_b = channels // groups_b
    weights = masked_weights(coupling, pattern)
    radial_cells = radial.reshape(KTERMS, cells).T
    for _ in range(STEPS):
        flat = amplitude.reshape(2 * cells, channels)
        applied = jnp.einsum("mj,kij->mki", flat, weights, preferred_element_type=jnp.float32)
        applied = applied.reshape(2, cells, KTERMS, channels)
        coupled = jnp.sum(applied * radial_cells[None, :, :, None], axis=2)
        wide = amplitude.reshape(2, cells, channels).astype(jnp.float32)
        kicked = jnp.stack([wide[0] + coupled[1], wide[1] - coupled[0]]).astype(jnp.bfloat16)
        grouped = kicked.reshape(2, first_rows, second_rows, groups_a, width_a)
        grouped = grouped.transpose(0, 1, 3, 2, 4).reshape(
            2, first_rows, groups_a, second_rows * width_a
        )
        half = complex_rows(
            first_prop, lax.all_to_all(grouped, "ra", split_axis=2, concat_axis=1, tiled=True)
        )
        restored = lax.all_to_all(half, "ra", split_axis=1, concat_axis=2, tiled=True)
        restored = restored.reshape(2, first_rows, groups_a, second_rows, width_a)
        restored = restored.transpose(0, 1, 3, 2, 4).reshape(
            2, first_rows, second_rows, groups_b, width_b
        )
        regrouped = restored.transpose(0, 2, 3, 1, 4).reshape(
            2, second_rows, groups_b, first_rows * width_b
        )
        moved = complex_rows(
            second_prop, lax.all_to_all(regrouped, "rb", split_axis=2, concat_axis=1, tiled=True)
        )
        settled = lax.all_to_all(moved, "rb", split_axis=1, concat_axis=2, tiled=True)
        settled = settled.reshape(2, second_rows, groups_b, first_rows, width_b)
        amplitude = settled.transpose(0, 3, 1, 2, 4).reshape(2, first_rows, second_rows, channels)
    return amplitude


def prop_kernel(turned, n_in, n_out, mat_ref, *refs):
    ins, outs, rest = refs[:n_in], refs[n_in:n_in + n_out], refs[n_in + n_out:]
    depth = mat_ref.shape[1]
    outer = ins[0].shape[1]
    rows = depth // n_out
    step = pl.program_id(0)

    def one(o, carry):
        real = jnp.concatenate([r[0, o] for r in ins], axis=0)
        imag = jnp.concatenate([r[1, o] for r in ins], axis=0)
        res = jnp.dot(
            mat_ref[0], jnp.concatenate([real, imag], axis=1), preferred_element_type=jnp.float32
        ) + jnp.dot(
            mat_ref[1], jnp.concatenate([-imag, real], axis=1), preferred_element_type=jnp.float32
        )
        if turned:
            for p in range(2):
                rest[0][p, pl.ds(step * outer + o, depth, stride=TILE), :] = res[:, p * LANES:(p + 1) * LANES]
        else:
            for p in range(2):
                for s in range(n_out):
                    outs[s][p, o] = res[s * rows:(s + 1) * rows, p * LANES:(p + 1) * LANES].astype(jnp.bfloat16)
        return carry

    lax.fori_loop(0, outer, one, 0)
    if turned:
        @pl.when(step == pl.num_programs(0) - 1)
        def _():
            span = rows * TILE
            for p in range(2):
                for s in range(n_out):
                    outs[s][p] = rest[0][p, s * span:(s + 1) * span, :].reshape(rows, TILE, LANES).astype(jnp.bfloat16)


def propagate(matrix, pieces, place, n_out, turned):
    depth = matrix.shape[1]
    rows = depth // n_out
    outer = 4
    parts = TILE // outer
    in_specs = [pl.BlockSpec(matrix.shape, lambda g: (0, 0, 0))] + [
        pl.BlockSpec((2, outer, p.shape[2], LANES), lambda g: (0, place * parts + g, 0, 0)) for p in pieces
    ]
    if turned:
        shape = (2, rows, TILE, LANES)
        out_specs = [pl.BlockSpec(shape, lambda g: (0, 0, 0, 0))] * n_out
        scratch = [pltpu.VMEM((2, depth * TILE, LANES), jnp.float32)]
    else:
        shape = (2, TILE, rows, LANES)
        out_specs = [pl.BlockSpec((2, outer, rows, LANES), lambda g: (0, g, 0, 0))] * n_out
        scratch = []
    return pl.pallas_call(
        functools.partial(prop_kernel, turned, len(pieces), n_out),
        grid=(parts,),
        in_specs=in_specs,
        out_specs=out_specs,
        out_shape=[jax.ShapeDtypeStruct(shape, jnp.bfloat16)] * n_out,
        scratch_shapes=scratch,
        cost_estimate=pl.CostEstimate(
            flops=8 * depth * depth * TILE * LANES, bytes_accessed=8 * depth * TILE * LANES, transcendentals=0
        ),
        compiler_params=pltpu.CompilerParams(vmem_limit_bytes=56 * 2**20),
    )(matrix, *pieces)


def kick_rows(planes, old, weights, factor):
    coupled = []
    for p in range(2):
        applied = jnp.dot(planes[p], weights, preferred_element_type=jnp.float32)
        total = applied[:, :LANES] * factor[:, 0:1]
        for k in range(1, KTERMS):
            total = total + applied[:, k * LANES:(k + 1) * LANES] * factor[:, k:k + 1]
        coupled.append(total)
    return old[0].astype(jnp.float32) + coupled[1], old[1].astype(jnp.float32) - coupled[0]


def kick_turned_kernel(where_ref, amp_ref, weights_ref, factor_ref, *outs):
    a_rows, b_rows = amp_ref.shape[1], amp_ref.shape[2]
    count = a_rows * b_rows
    planes = [amp_ref[p].reshape(count, amp_ref.shape[3]) for p in range(2)]
    factor = factor_ref[...].reshape(count, KTERMS)
    for s in range(2):
        low = where_ref[1] == s
        old = [jnp.where(low, p[:, :LANES], p[:, LANES:]) for p in planes]
        result = kick_rows(planes, old, weights_ref[s], factor)
        for p in range(2):
            outs[s][p] = jnp.swapaxes(result[p].reshape(a_rows, b_rows, LANES), 0, 1).astype(jnp.bfloat16)


def kick_turned(amplitude, weights, factor, where):
    a_rows, channels = amplitude.shape[1], amplitude.shape[3]
    shape = jax.ShapeDtypeStruct((2, TILE, a_rows, LANES), jnp.bfloat16)
    spec = pltpu.PrefetchScalarGridSpec(
        num_scalar_prefetch=1,
        grid=(a_rows // TILE,),
        in_specs=[
            pl.BlockSpec((2, TILE, TILE, channels), lambda g, w: (0, g, w[0], 0)),
            pl.BlockSpec(weights.shape, lambda g, w: (0, 0, 0)),
            pl.BlockSpec((TILE, TILE, KTERMS), lambda g, w: (g, w[0], 0)),
        ],
        out_specs=[pl.BlockSpec((2, TILE, TILE, LANES), lambda g, w: (0, 0, g, 0))] * 2,
    )
    return pl.pallas_call(
        kick_turned_kernel,
        grid_spec=spec,
        out_shape=[shape, shape],
        cost_estimate=pl.CostEstimate(
            flops=8 * TILE * a_rows * channels * KTERMS * LANES,
            bytes_accessed=8 * TILE * a_rows * channels, transcendentals=0,
        ),
    )(where, amplitude, weights, factor)


def kick_pair_kernel(own_ref, other_ref, weights_ref, factor_ref, own_out, other_out):
    halves = [[ref[p, 0] for p in range(2)] for ref in (own_ref, other_ref)]
    planes = [jnp.concatenate([halves[0][p], halves[1][p]], axis=1) for p in range(2)]
    factor = factor_ref[0]
    for s, out in enumerate((own_out, other_out)):
        result = kick_rows(planes, halves[s], weights_ref[s], factor)
        for p in range(2):
            out[p, 0] = result[p].astype(jnp.bfloat16)


def kick_pair(own, other, weights, factor, place):
    a_rows, b_rows = own.shape[1], own.shape[2]
    block = pl.BlockSpec((2, 1, b_rows, LANES), lambda g: (0, g, 0, 0))
    shape = jax.ShapeDtypeStruct(own.shape, jnp.bfloat16)
    return pl.pallas_call(
        kick_pair_kernel,
        grid=(a_rows,),
        in_specs=[
            block, block,
            pl.BlockSpec(weights.shape, lambda g: (0, 0, 0)),
            pl.BlockSpec((1, b_rows, KTERMS), lambda g: (place * a_rows + g, 0, 0)),
        ],
        out_specs=[block, block],
        out_shape=[shape, shape],
        cost_estimate=pl.CostEstimate(
            flops=4 * a_rows * b_rows * 4 * LANES * KTERMS * LANES,
            bytes_accessed=16 * a_rows * b_rows * LANES, transcendentals=0,
        ),
    )(own, other, weights, factor)


def join_kernel(where_ref, own_ref, other_ref, *refs):
    low = where_ref[1] == 0
    own, other = own_ref[...], other_ref[...]
    refs[-1][:, :, :, :LANES] = jnp.where(low, own, other)
    refs[-1][:, :, :, LANES:] = jnp.where(low, other, own)


def join(own, other, into, where, shape):
    a_rows = own.shape[1]
    step = 32
    have = into is not None
    spec = pltpu.PrefetchScalarGridSpec(
        num_scalar_prefetch=1,
        grid=(a_rows // step,),
        in_specs=[pl.BlockSpec((2, step, TILE, LANES), lambda g, w: (0, g, 0, 0))] * 2
        + ([pl.BlockSpec(memory_space=pl.ANY)] if have else []),
        out_specs=pl.BlockSpec((2, step, TILE, 2 * LANES), lambda g, w: (0, g, w[0], 0)),
    )
    return pl.pallas_call(
        join_kernel,
        grid_spec=spec,
        out_shape=jax.ShapeDtypeStruct(shape, jnp.bfloat16),
        input_output_aliases={3: 0} if have else {},
        cost_estimate=pl.CostEstimate(flops=0, bytes_accessed=8 * own.size, transcendentals=0),
    )(where, own, other, *((into,) if have else ()))


def picks(index):
    full = index.shape[0]
    return (index[:, None] == jnp.arange(full)[None, :]).astype(jnp.bfloat16)


def arranged(matrix, rows, columns):
    first = jnp.einsum("rs,xst->xrt", picks(rows), matrix, preferred_element_type=jnp.float32)
    return jnp.einsum(
        "xrt,ct->xrc", first.astype(jnp.bfloat16), picks(columns), preferred_element_type=jnp.float32
    ).astype(jnp.bfloat16)


def on_device(amplitude, coupling, pattern, radial, first_prop, second_prop):
    a_rows, b_rows, channels = amplitude.shape[1:]
    n_a, n_b = first_prop.shape[1], second_prop.shape[1]
    ra, rb = lax.axis_size("ra"), lax.axis_size("rb")
    far = ra // 2 * rb
    a_far, b_far = n_a // far, n_b // far
    fits = (
        channels == 2 * LANES and ra % 2 == 0 and a_rows % TILE == 0
        and a_far % TILE == 0 and b_far % TILE == 0 and far & (far - 1) == 0
        and far <= 16
    )
    if not fits:
        return plain(amplitude, coupling, pattern, radial, first_prop, second_prop)

    at_a, at_b = lax.axis_index("ra"), lax.axis_index("rb")
    outer, half = at_a // 2, at_a % 2
    spot = outer * rb + at_b
    axes = ("ra", "rb")
    index = lambda ia, ib: ia * rb + ib

    def send_near(piece, s):
        if s == 0:
            return piece
        return lax.ppermute(piece, axes, [(index(i, j), index(i ^ s, j)) for i in range(ra) for j in range(rb)])

    def send_far(piece, s):
        if s == 0:
            return piece
        pairs = []
        for i in range(ra):
            for j in range(rb):
                to = ((i // 2) * rb + j) ^ s
                pairs.append((index(i, j), index((to // rb) * 2 + i % 2, to % rb)))
        return lax.ppermute(piece, axes, pairs)

    half_far, half_rb, half_b = a_far // 2, rb // 2, n_b // 2
    ia, ib = jnp.arange(n_a), jnp.arange(n_b)
    peer = spot ^ (ia // a_far)
    t = ia % a_far
    far_a = (peer // rb) * 2 * a_rows + (t // half_far) * a_rows + (peer % rb) * half_far + t % half_far
    peer = spot ^ (ib // b_far)
    far_b = (peer % rb) * b_rows + (peer // rb) * b_far + ib % b_far
    near_a = (at_a ^ (ia // a_rows)) * a_rows + ia % a_rows
    near_b = (half ^ (ib // half_b)) * half_b + ib % half_b

    first_out = arranged(first_prop, far_a, near_a)
    second_in = arranged(second_prop, near_b, far_b)
    second_out = arranged(second_prop, far_b, near_b)
    first_back = arranged(first_prop, near_a, far_a)

    weights = masked_weights(coupling, pattern).reshape(KTERMS, 2, LANES, channels)
    weights = weights.transpose(1, 3, 0, 2).reshape(2, channels, KTERMS * LANES)
    weights = jnp.where(half == 0, weights, weights[::-1])
    near_radial = radial.transpose(1, 2, 0)

    b_parts, a_parts = b_far // TILE, a_far // TILE

    def block_of(s, part):
        return jnp.stack([(outer ^ s) * b_parts + part, half]).astype(jnp.int32)

    kicks = []
    for part in range(b_parts):
        made = [None] * ra
        for s in reversed(range(ra // 2)):
            made[2 * s], made[2 * s + 1] = kick_turned(amplitude, weights, near_radial, block_of(s, part))
        kicks.append(made)
    later_radial = lax.optimization_barrier((radial, kicks[-1]))[0]

    got = []
    for u in range(rb):
        pairs = []
        for i in range(ra):
            for j in range(rb):
                to = ((i % 2) * half_rb + j % half_rb) ^ u
                pairs.append((index(i, j), index(i // 2 * 2 + j // half_rb, to)))
        to = (half * half_rb + at_b % half_rb) ^ u
        piece = lax.dynamic_slice_in_dim(later_radial, to * half_far, half_far, axis=1)
        got.append(lax.ppermute(piece, axes, pairs))

    halves, held = [], []
    for part in range(b_parts):
        made = kicks[part]
        if part:
            made = lax.optimization_barrier((made, pieces))[0]
        pieces = [send_near(made[s], s) for s in range(ra)]
        spread = propagate(first_out, pieces, 0, far * a_parts, True)
        held.append([spread[p::a_parts] for p in range(a_parts)])
    for p in range(a_parts):
        for part in range(b_parts):
            sent = held[part][p]
            halves.append([send_far(h, s) for s, h in enumerate(sent)])
    halves = [halves[p * b_parts:(p + 1) * b_parts] for p in range(a_parts)]

    turned = weights.reshape(2, 2, LANES, KTERMS * LANES)
    turned = jnp.where(half == 0, turned, turned[:, ::-1]).reshape(weights.shape)
    ordered = jnp.stack(got)
    for bit in range(rb.bit_length() - 1):
        pairs = ordered.reshape(rb >> (bit + 1), 2, 1 << bit, *got[0].shape)
        pairs = jnp.where((at_b >> bit) % 2 == 0, pairs, pairs[:, ::-1])
        ordered = pairs.reshape(rb, *got[0].shape)
    ordered = ordered.reshape(2, half_rb, KTERMS, half_far, b_rows)
    far_radial = ordered.transpose(0, 3, 1, 4, 2).reshape(a_far, half_b, KTERMS)
    back = []
    for part in range(a_parts):
        gathered = [halves[part][q][s] for s in range(far) for q in range(b_parts)]
        own, other = propagate(second_in, gathered, 0, 2, False)
        other = send_near(other, 1)
        own, other = kick_pair(own, other, turned, far_radial, part)
        other = send_near(other, 1)
        spread = propagate(second_out, [own, other], 0, far, True)
        back.append([send_far(h, s) for s, h in enumerate(spread)])
    gathered = [back[part][s] for s in range(far) for part in range(a_parts)]

    result = None
    for part in range(b_parts):
        moved = propagate(first_back, gathered, part, ra, True)
        moved = [send_near(piece, s) for s, piece in enumerate(moved)]
        for s in range(ra // 2):
            result = join(moved[2 * s], moved[2 * s + 1], result, block_of(s, part), amplitude.shape)
    return result


def solution(mesh):
    return jax.shard_map(
        on_device,
        mesh=mesh,
        in_specs=(P(None, "ra", "rb", None), P(), P(), P(None, "ra", "rb"), P(), P()),
        out_specs=P(None, "ra", "rb", None),
        check_vma=False,
    )
```

profile of v0, /device:TPU:0, one launch (start us, length us, event | category | flops | bytes accessed | tf_op | source)
XLA Modules:
  0.0 715.8 jit_solution(15732143743685906303)
XLA Ops:
  4.7 4.4 copy.32
  10.9 9.4 %shard_map.65 = (bf16[2,16,128,128]{3,2,1,0:T(8,128)(2,1)}, bf16[2,16,128,128]{3,2,1,0:T(8,128)(2,1)}) custom-call(s32[2]{0:T(128)} %get-tuple-element.269.where_ref, bf16[2,128,64,256]{3,2,1,0:T(8,128)(2,1)} %amp_ref.7, bf16[2,256,768]{2,1,0:T(8,128)(2,1)} %reverse_select_fusion.3.weights_ref, f32[128,64,6]{2,1,0:T(8,128)} %bitcast.76), custom_call_target="tpu_custom_call" | custom-call | flops 3221225472 | bytes 4194304 | tf_op jit(solution)/shard_map/pallas_call | solution.py:179
  23.9 9.4 %shard_map.64 = (bf16[2,16,128,128]{3,2,1,0:T(8,128)(2,1)}, bf16[2,16,128,128]{3,2,1,0:T(8,128)(2,1)}) custom-call(s32[2]{0:T(128)} %get-tuple-element.268.where_ref, bf16[2,128,64,256]{3,2,1,0:T(8,128)(2,1)} %amp_ref.7, bf16[2,256,768]{2,1,0:T(8,128)(2,1)} %reverse_select_fusion.3.weights_ref, f32[128,64,6]{2,1,0:T(8,128)} %bitcast.77), custom_call_target="tpu_custom_call" | custom-call | flops 3221225472 | bytes 4194304 | tf_op jit(solution)/shard_map/pallas_call | solution.py:179
  33.4 9.4 %shard_map.68 = (bf16[2,16,128,128]{3,2,1,0:T(8,128)(2,1)}, bf16[2,16,128,128]{3,2,1,0:T(8,128)(2,1)}) custom-call(s32[2]{0:T(128)} %get-tuple-element.267.where_ref, bf16[2,128,64,256]{3,2,1,0:T(8,128)(2,1)} %amp_ref.7, bf16[2,256,768]{2,1,0:T(8,128)(2,1)} %reverse_select_fusion.3.weights_ref, f32[128,64,6]{2,1,0:T(8,128)} %bitcast.78), custom_call_target="tpu_custom_call" | custom-call | flops 3221225472 | bytes 4194304 | tf_op jit(solution)/shard_map/pallas_call | solution.py:179
  42.8 9.5 %shard_map.67 = (bf16[2,16,128,128]{3,2,1,0:T(8,128)(2,1)}, bf16[2,16,128,128]{3,2,1,0:T(8,128)(2,1)}) custom-call(s32[2]{0:T(128)} %get-tuple-element.270.where_ref, bf16[2,128,64,256]{3,2,1,0:T(8,128)(2,1)} %amp_ref.7, bf16[2,256,768]{2,1,0:T(8,128)(2,1)} %reverse_select_fusion.3.weights_ref, f32[128,64,6]{2,1,0:T(8,128)} %bitcast.79), custom_call_target="tpu_custom_call" | custom-call | flops 3221225472 | bytes 4194304 | tf_op jit(solution)/shard_map/pallas_call | solution.py:179
  54.9 13.6 %collective-permute-done.2.refs_3_ = bf16[2,16,128,128]{3,2,1,0:T(8,128)(2,1)} collective-permute-done((bf16[2,16,128,128]{3,2,1,0:T(8,128)(2,1)}, bf16[2,16,128,128]{3,2,1,0:T(8,128)(2,1)}, u32[]{:S(2)}, u32[]{:S(2)}) %collective-permute-start.2) | collective-permute-done | bytes 1048608 | tf_op jit(solution)/shard_map/ppermute | solution.py:283
  68.4 14.0 %shard_map.66 = (bf16[2,16,16,128]{3,2,1,0:T(8,128)(2,1)}, bf16[2,16,16,128]{3,2,1,0:T(8,128)(2,1)}, bf16[2,16,16,128]{3,2,1,0:T(8,128)(2,1)}, bf16[2,16,16,128]...) custom-call(bf16[2,512,512]{2,1,0:T(8,128)(2,1)} %convolution_conver, ...), custom_call_target="tpu_custom_call" | custom-call | flops 4294967296 | bytes 8388608 | tf_op jit(solution)/shard_map/pallas_call | solution.py:128
  96.2 5.7 collective-permute-done.39
  101.9 4.1 collective-permute-done.38
  106.8 9.1 %collective-permute-start.14 = (bf16[2,16,16,128]{3,2,1,0:T(8,128)(2,1)}, bf16[2,16,16,128]{3,2,1,0:T(8,128)(2,1)S(1)}, u32[]{:S(2)}, u32[]{:S(2)}) collective-permute-start(bf16[2,16,16,128]{3,2,1,0:T(8,128)(2,1)} %get-tuple-element.152), channel_id=1, source_target_pairs={{0,5},{1,4},{2,7},{3,6},{4,1},{5,0},{6,3},{7,2},{8,13},{9,12},{10,... | collective-permute-start | bytes 393224 | tf_op jit(solution)/shard_map/ppermute | solution.py:293
  116.0 5.6 collective-permute-start.18
  123.2 4.8 collective-permute-done.14.refs_10_
  129.4 5.4 collective-permute-start.26
  143.3 6.3 collective-permute-done.28.refs_24_
  157.8 4.2 collective-permute-start.46
  167.7 4.2 collective-permute-done.48.refs_4_
  176.2 7.8 %collective-permute-done.52.refs_8_ = bf16[2,16,16,128]{3,2,1,0:T(8,128)(2,1)} collective-permute-done((bf16[2,16,16,128]{3,2,1,0:T(8,128)(2,1)}, bf16[2,16,16,128]{3,2,1,0:T(8,128)(2,1)}, u32[]{:S(2)}, u32[]{:S(2)}) %collective-permute-start.52) | collective-permute-done | bytes 131104 | tf_op jit(solution)/shard_map/ppermute | solution.py:293
  187.9 4.2 collective-permute-done.56.refs_12_
  195.4 3.5 collective-permute-start.66
  199.0 14.0 %shard_map.69 = (bf16[2,16,16,128]{3,2,1,0:T(8,128)(2,1)}, bf16[2,16,16,128]{3,2,1,0:T(8,128)(2,1)}, bf16[2,16,16,128]{3,2,1,0:T(8,128)(2,1)}, bf16[2,16,16,128]...) custom-call(bf16[2,512,512]{2,1,0:T(8,128)(2,1)} %convolution_conver, ...), custom_call_target="tpu_custom_call" | custom-call | flops 4294967296 | bytes 8388608 | tf_op jit(solution)/shard_map/pallas_call | solution.py:128
  218.8 4.0 collective-permute-start.74
  223.8 8.7 %collective-permute-done.68.refs_24_ = bf16[2,16,16,128]{3,2,1,0:T(8,128)(2,1)S(1)} collective-permute-done((bf16[2,16,16,128]{3,2,1,0:T(8,128)(2,1)S(1)}, bf16[2,16,16,128]{3,2,1,0:T(8,128)(2,1)S(1)}, u32[]{:S(2)}, u32[]{:S(2)}) %collective-permute-start.68) | collective-permute-done | bytes 131104 | tf_op jit(solution)/shard_map/ppermute | solution.py:293
  238.2 5.4 collective-permute-start.15
  249.1 6.4 collective-permute-done.15.refs_11_
  263.6 7.2 %collective-permute-start.61 = (bf16[2,16,16,128]{3,2,1,0:T(8,128)(2,1)}, bf16[2,16,16,128]{3,2,1,0:T(8,128)(2,1)S(1)}, u32[]{:S(2)}, u32[]{:S(2)}) collective-permute-start(bf16[2,16,16,128]{3,2,1,0:T(8,128)(2,1)} %get-tuple-element.197), channel_id=1, source_target_pairs={{0,16},{1,17},{2,18},{3,19},{4,20},{5,21},{6,22},{7,23},{8,24},{9,... | collective-permute-start | bytes 393224 | tf_op jit(solution)/shard_map/ppermute | solution.py:293
  271.3 4.2 collective-permute-start.63
  278.6 4.1 collective-permute-start.69
  283.3 4.2 collective-permute-done.63.refs_19_
  287.8 4.6 collective-permute-start.75
  292.5 8.7 %collective-permute-done.69.refs_25_ = bf16[2,16,16,128]{3,2,1,0:T(8,128)(2,1)S(1)} collective-permute-done((bf16[2,16,16,128]{3,2,1,0:T(8,128)(2,1)}, bf16[2,16,16,128]{3,2,1,0:T(8,128)(2,1)S(1)}, u32[]{:S(2)}, u32[]{:S(2)}) %collective-permute-start.69) | collective-permute-done | bytes 131104 | tf_op jit(solution)/shard_map/ppermute | solution.py:293
  306.6 4.2 collective-permute-start.27
  311.1 10.7 %shard_map.73 = (bf16[2,16,256,128]{3,2,1,0:T(8,128)(2,1)}, bf16[2,16,256,128]{3,2,1,0:T(8,128)(2,1)}) custom-call(bf16[2,512,512]{2,1,0:T(8,128)(2,1)} %convolution_convert_fusion.2.mat_ref, bf16[2,16,16,128]{3,2,1,0:T(8,128)(2,1)} %get-tuple-element.180.refs_0_, bf16[2,16,16,128]{3,2,1,0:T(8,128)(2,1)} %get-tuple-element.181.refs_1_, ...), custom_call_target="tpu_custom_call" | custom-call | flops 4294967296 | bytes 8388608 | tf_op jit(solution)/shard_map/pallas_call | solution.py:128
  331.6 7.0 collective-permute-done.29.refs_25_
  345.5 10.7 %shard_map.70 = (bf16[2,16,256,128]{3,2,1,0:T(8,128)(2,1)}, bf16[2,16,256,128]{3,2,1,0:T(8,128)(2,1)}) custom-call(bf16[2,512,512]{2,1,0:T(8,128)(2,1)} %convolution_convert_fusion.2.mat_ref, bf16[2,16,16,128]{3,2,1,0:T(8,128)(2,1)} %get-tuple-element.134.refs_0_, bf16[2,16,16,128]{3,2,1,0:T(8,128)(2,1)} %get-tuple-element.143.refs_1_, ...), custom_call_target="tpu_custom_call" | custom-call | flops 4294967296 | bytes 8388608 | tf_op jit(solution)/shard_map/pallas_call | solution.py:128
  359.1 4.4 reverse_select_fusion.1
  366.0 15.8 %shard_map.74 = (bf16[2,16,256,128]{3,2,1,0:T(8,128)(2,1)}, bf16[2,16,256,128]{3,2,1,0:T(8,128)(2,1)}) custom-call(bf16[2,16,256,128]{3,2,1,0:T(8,128)(2,1)} %get-tuple-element.212.own_ref, bf16[2,16,256,128]{3,2,1,0:T(8,128)(2,1)} %collective-permute-done.76.other_ref, bf16[2,256,768]{2,1,0:T(8,128)(2,1)} %bitcast.87, f32[32,256,6]{2,1,0:T(8,128)} %bitcast.82), custom_call_target="tpu_custom_call" | custom-call | flops 6442450944 | bytes 8388608 | tf_op jit(solution)/shard_map/pallas_call | solution.py:204
  382.2 15.8 %shard_map.71 = (bf16[2,16,256,128]{3,2,1,0:T(8,128)(2,1)}, bf16[2,16,256,128]{3,2,1,0:T(8,128)(2,1)}) custom-call(bf16[2,16,256,128]{3,2,1,0:T(8,128)(2,1)} %get-tuple-element.174.own_ref, bf16[2,16,256,128]{3,2,1,0:T(8,128)(2,1)} %collective-permute-done.36.other_ref, bf16[2,256,768]{2,1,0:T(8,128)(2,1)} %bitcast.88, f32[32,256,6]{2,1,0:T(8,128)} %bitcast.83), custom_call_target="tpu_custom_call" | custom-call | flops 6442450944 | bytes 8388608 | tf_op jit(solution)/shard_map/pallas_call | solution.py:204
  401.7 13.8 %shard_map.75 = (bf16[2,32,16,128]{3,2,1,0:T(8,128)(2,1)}, bf16[2,32,16,128]{3,2,1,0:T(8,128)(2,1)}, bf16[2,32,16,128]{3,2,1,0:T(8,128)(2,1)}, bf16[2,32,16,128]...) custom-call(bf16[2,512,512]{2,1,0:T(8,128)(2,1)} %convolution_conver, ...), custom_call_target="tpu_custom_call" | custom-call | flops 4294967296 | bytes 8388608 | tf_op jit(solution)/shard_map/pallas_call | solution.py:128
  416.3 4.2 collective-permute-start.81
  425.9 10.5 %collective-permute-done.81.refs_5_ = bf16[2,32,16,128]{3,2,1,0:T(8,128)(2,1)S(1)} collective-permute-done((bf16[2,32,16,128]{3,2,1,0:T(8,128)(2,1)}, bf16[2,32,16,128]{3,2,1,0:T(8,128)(2,1)S(1)}, u32[]{:S(2)}, u32[]{:S(2)}) %collective-permute-start.81) | collective-permute-done | bytes 262176 | tf_op jit(solution)/shard_map/ppermute | solution.py:293
  444.4 19.1 %collective-permute-done.87.refs_11_ = bf16[2,32,16,128]{3,2,1,0:T(8,128)(2,1)S(1)} collective-permute-done((bf16[2,32,16,128]{3,2,1,0:T(8,128)(2,1)}, bf16[2,32,16,128]{3,2,1,0:T(8,128)(2,1)S(1)}, u32[]{:S(2)}, u32[]{:S(2)}) %collective-permute-start.87) | collective-permute-done | bytes 262176 | tf_op jit(solution)/shard_map/ppermute | solution.py:293
  463.6 6.0 collective-permute-start.99
  469.6 6.2 collective-permute-start.101
  476.2 4.4 collective-permute-start.105
  481.6 13.9 %shard_map.72 = (bf16[2,32,16,128]{3,2,1,0:T(8,128)(2,1)}, bf16[2,32,16,128]{3,2,1,0:T(8,128)(2,1)}, bf16[2,32,16,128]{3,2,1,0:T(8,128)(2,1)}, bf16[2,32,16,128]...) custom-call(bf16[2,512,512]{2,1,0:T(8,128)(2,1)} %convolution_conver, ...), custom_call_target="tpu_custom_call" | custom-call | flops 4294967296 | bytes 8388608 | tf_op jit(solution)/shard_map/pallas_call | solution.py:128
  497.4 8.0 %collective-permute-done.101.refs_25_ = bf16[2,32,16,128]{3,2,1,0:T(8,128)(2,1)} collective-permute-done((bf16[2,32,16,128]{3,2,1,0:T(8,128)(2,1)}, bf16[2,32,16,128]{3,2,1,0:T(8,128)(2,1)}, u32[]{:S(2)}, u32[]{:S(2)}) %collective-permute-start.101) | collective-permute-done | bytes 262176 | tf_op jit(solution)/shard_map/ppermute | solution.py:293
  505.4 5.7 collective-permute-done.103.refs_27_
  511.1 7.2 %collective-permute-start.84 = (bf16[2,32,16,128]{3,2,1,0:T(8,128)(2,1)}, bf16[2,32,16,128]{3,2,1,0:T(8,128)(2,1)S(1)}, u32[]{:S(2)}, u32[]{:S(2)}) collective-permute-start(bf16[2,32,16,128]{3,2,1,0:T(8,128)(2,1)} %get-tuple-element.223), channel_id=1, source_target_pairs={{0,4},{1,5},{2,6},{3,7},{4,0},{5,1},{6,2},{7,3},{8,12},{9,13},{10,... | collective-permute-start | bytes 786440 | tf_op jit(solution)/shard_map/ppermute | solution.py:293
  518.4 17.7 %collective-permute-start.86 = (bf16[2,32,16,128]{3,2,1,0:T(8,128)(2,1)}, bf16[2,32,16,128]{3,2,1,0:T(8,128)(2,1)S(1)}, u32[]{:S(2)}, u32[]{:S(2)}) collective-permute-start(bf16[2,32,16,128]{3,2,1,0:T(8,128)(2,1)} %get-tuple-element.225), channel_id=1, source_target_pairs={{0,5},{1,4},{2,7},{3,6},{4,1},{5,0},{6,3},{7,2},{8,13},{9,12},{10,... | collective-permute-start | bytes 786440 | tf_op jit(solution)/shard_map/ppermute | solution.py:293
  544.0 6.7 collective-permute-done.84.refs_8_
  550.7 5.7 collective-permute-done.86.refs_10_
  556.4 5.8 collective-permute-start.98
  562.3 6.3 collective-permute-start.100
  579.3 18.3 %collective-permute-done.100.refs_24_ = bf16[2,32,16,128]{3,2,1,0:T(8,128)(2,1)} collective-permute-done((bf16[2,32,16,128]{3,2,1,0:T(8,128)(2,1)}, bf16[2,32,16,128]{3,2,1,0:T(8,128)(2,1)}, u32[]{:S(2)}, u32[]{:S(2)}) %collective-permute-start.100) | collective-permute-done | bytes 262176 | tf_op jit(solution)/shard_map/ppermute | solution.py:293
  597.6 6.5 collective-permute-done.102.refs_26_
  604.0 14.4 %shard_map.77 = (bf16[2,128,16,128]{3,2,1,0:T(8,128)(2,1)}, bf16[2,128,16,128]{3,2,1,0:T(8,128)(2,1)}, bf16[2,128,16,128]{3,2,1,0:T(8,128)(2,1)}, bf16[2,128,16,128]{3,2,1,0:T(8,128)(2,1)}) custom-call(bf16[2,512,512]{2,1,0:T(8,128)(2,1)} %convolution_convert_fusion.6.mat_ref, bf16[2,32,16,128]{3,2,1,0:T(8,128)(2,1)} %get-tuple-element.179.refs_0_, ...), custom_call_target="tpu_custom_call" | custom-call | flops 4294967296 | bytes 8388608 | tf_op jit(solution)/shard_map/pallas_call | solution.py:128
  620.4 14.4 %shard_map.76 = (bf16[2,128,16,128]{3,2,1,0:T(8,128)(2,1)}, bf16[2,128,16,128]{3,2,1,0:T(8,128)(2,1)}, bf16[2,128,16,128]{3,2,1,0:T(8,128)(2,1)}, bf16[2,128,16,128]{3,2,1,0:T(8,128)(2,1)}) custom-call(bf16[2,512,512]{2,1,0:T(8,128)(2,1)} %convolution_convert_fusion.6.mat_ref, bf16[2,32,16,128]{3,2,1,0:T(8,128)(2,1)} %get-tuple-element.179.refs_0_, ...), custom_call_target="tpu_custom_call" | custom-call | flops 4294967296 | bytes 8388608 | tf_op jit(solution)/shard_map/pallas_call | solution.py:128
  637.8 4.5 shard_map.78.refs_0_
  644.8 21.7 %collective-permute-done.112.other_ref = bf16[2,128,16,128]{3,2,1,0:T(8,128)(2,1)} collective-permute-done((bf16[2,128,16,128]{3,2,1,0:T(8,128)(2,1)}, bf16[2,128,16,128]{3,2,1,0:T(8,128)(2,1)}, u32[]{:S(2)}, u32[]{:S(2)}) %collective-permute-start.112) | collective-permute-done | bytes 1048608 | tf_op jit(solution)/shard_map/ppermute | solution.py:283
  666.5 4.5 shard_map.79.refs_0_
  671.1 4.5 shard_map.80.refs_0_
  675.6 14.3 %collective-permute-done.108.own_ref = bf16[2,128,16,128]{3,2,1,0:T(8,128)(2,1)} collective-permute-done((bf16[2,128,16,128]{3,2,1,0:T(8,128)(2,1)}, bf16[2,128,16,128]{3,2,1,0:T(8,128)(2,1)}, u32[]{:S(2)}, u32[]{:S(2)}) %collective-permute-start.108) | collective-permute-done | bytes 1048608 | tf_op jit(solution)/shard_map/ppermute | solution.py:283
  689.9 21.4 %collective-permute-done.109.other_ref = bf16[2,128,16,128]{3,2,1,0:T(8,128)(2,1)} collective-permute-done((bf16[2,128,16,128]{3,2,1,0:T(8,128)(2,1)}, bf16[2,128,16,128]{3,2,1,0:T(8,128)(2,1)}, u32[]{:S(2)}, u32[]{:S(2)}) %collective-permute-start.109) | collective-permute-done | bytes 1048608 | tf_op jit(solution)/shard_map/ppermute | solution.py:283
  711.3 4.5 shard_map.81
  (396 shorter events, 169.8 us)
Async XLA Ops:
  20.3 34.6 %collective-permute-start.1 = (bf16[2,16,128,128]{3,2,1,0:T(8,128)(2,1)}, bf16[2,16,128,128]{3,2,1,0:T(8,128)(2,1)}, u32[]{:S(2)}, u32[]{:S(2)}) collective-permute-start(bf16[2,16,128,128]{3,2,1,0:T(8,128)(2,1)} %get-tuple-element.132), channel_id=1, source_target_pairs={{0,16},{1,17},{2,18},{3,19},{4,20},{5,21},{6,22},{7,23},{8,24},{9,... | collective-permute-start | bytes 3145736 | tf_op jit(solution)/shard_map/ppermute | solution.py:283
  23.2 45.2 %collective-permute-start.2 = (bf16[2,16,128,128]{3,2,1,0:T(8,128)(2,1)}, bf16[2,16,128,128]{3,2,1,0:T(8,128)(2,1)}, u32[]{:S(2)}, u32[]{:S(2)}) collective-permute-start(bf16[2,16,128,128]{3,2,1,0:T(8,128)(2,1)} %get-tuple-element.133), channel_id=1, source_target_pairs={{0,24},{1,25},{2,26},{3,27},{4,28},{5,29},{6,30},{7,31},{8,16},{9,... | collective-permute-start | bytes 3145736 | tf_op jit(solution)/shard_map/ppermute | solution.py:283
  33.3 35.2 %collective-permute-start = (bf16[2,16,128,128]{3,2,1,0:T(8,128)(2,1)}, bf16[2,16,128,128]{3,2,1,0:T(8,128)(2,1)}, u32[]{:S(2)}, u32[]{:S(2)}) collective-permute-start(bf16[2,16,128,128]{3,2,1,0:T(8,128)(2,1)} %get-tuple-element.131), channel_id=1, source_target_pairs={{0,8},{1,9},{2,10},{3,11},{4,12},{5,13},{6,14},{7,15},{8,0},{9,1},... | collective-permute-start | bytes 3145736 | tf_op jit(solution)/shard_map/ppermute | solution.py:283
  82.4 33.5 %collective-permute-start.6 = (bf16[2,16,16,128]{3,2,1,0:T(8,128)(2,1)}, bf16[2,16,16,128]{3,2,1,0:T(8,128)(2,1)S(1)}, u32[]{:S(2)}, u32[]{:S(2)}) collective-permute-start(bf16[2,16,16,128]{3,2,1,0:T(8,128)(2,1)} %get-tuple-element.144), channel_id=1, source_target_pairs={{0,1},{1,0},{2,3},{3,2},{4,5},{5,4},{6,7},{7,6},{8,9},{9,8},{10,11... | collective-permute-start | bytes 393224 | tf_op jit(solution)/shard_map/ppermute | solution.py:293
  89.9 26.1 %collective-permute-start.8 = (bf16[2,16,16,128]{3,2,1,0:T(8,128)(2,1)}, bf16[2,16,16,128]{3,2,1,0:T(8,128)(2,1)S(1)}, u32[]{:S(2)}, u32[]{:S(2)}) collective-permute-start(bf16[2,16,16,128]{3,2,1,0:T(8,128)(2,1)} %get-tuple-element.146), channel_id=1, source_target_pairs={{0,2},{1,3},{2,0},{3,1},{4,6},{5,7},{6,4},{7,5},{8,10},{9,11},{10,... | collective-permute-start | bytes 393224 | tf_op jit(solution)/shard_map/ppermute | solution.py:293
  90.3 31.3 %collective-permute-start.10 = (bf16[2,16,16,128]{3,2,1,0:T(8,128)(2,1)}, bf16[2,16,16,128]{3,2,1,0:T(8,128)(2,1)S(1)}, u32[]{:S(2)}, u32[]{:S(2)}) collective-permute-start(bf16[2,16,16,128]{3,2,1,0:T(8,128)(2,1)} %get-tuple-element.148), channel_id=1, source_target_pairs={{0,3},{1,2},{2,1},{3,0},{4,7},{5,6},{6,5},{7,4},{8,11},{9,10},{10,... | collective-permute-start | bytes 393224 | tf_op jit(solution)/shard_map/ppermute | solution.py:293
  92.7 30.5 %collective-permute-start.12 = (bf16[2,16,16,128]{3,2,1,0:T(8,128)(2,1)}, bf16[2,16,16,128]{3,2,1,0:T(8,128)(2,1)S(1)}, u32[]{:S(2)}, u32[]{:S(2)}) collective-permute-start(bf16[2,16,16,128]{3,2,1,0:T(8,128)(2,1)} %get-tuple-element.150), channel_id=1, source_target_pairs={{0,4},{1,5},{2,6},{3,7},{4,0},{5,1},{6,2},{7,3},{8,12},{9,13},{10,... | collective-permute-start | bytes 393224 | tf_op jit(solution)/shard_map/ppermute | solution.py:293
  106.8 21.2 %collective-permute-start.14 = (bf16[2,16,16,128]{3,2,1,0:T(8,128)(2,1)}, bf16[2,16,16,128]{3,2,1,0:T(8,128)(2,1)S(1)}, u32[]{:S(2)}, u32[]{:S(2)}) collective-permute-start(bf16[2,16,16,128]{3,2,1,0:T(8,128)(2,1)} %get-tuple-element.152), channel_id=1, source_target_pairs={{0,5},{1,4},{2,7},{3,6},{4,1},{5,0},{6,3},{7,2},{8,13},{9,12},{10,... | collective-permute-start | bytes 393224 | tf_op jit(solution)/shard_map/ppermute | solution.py:293
  134.8 58.6 %collective-permute-start.3 = (bf16[2,16,128,128]{3,2,1,0:T(8,128)(2,1)}, bf16[2,16,128,128]{3,2,1,0:T(8,128)(2,1)}, u32[]{:S(2)}, u32[]{:S(2)}) collective-permute-start(bf16[2,16,128,128]{3,2,1,0:T(8,128)(2,1)} %get-tuple-element.140), channel_id=1, source_target_pairs={{0,8},{1,9},{2,10},{3,11},{4,12},{5,13},{6,14},{7,15},{8,0},{9,1},... | collective-permute-start | bytes 3145736 | tf_op jit(solution)/shard_map/ppermute | solution.py:283
  134.8 58.6 %collective-permute-start.4 = (bf16[2,16,128,128]{3,2,1,0:T(8,128)(2,1)}, bf16[2,16,128,128]{3,2,1,0:T(8,128)(2,1)}, u32[]{:S(2)}, u32[]{:S(2)}) collective-permute-start(bf16[2,16,128,128]{3,2,1,0:T(8,128)(2,1)} %get-tuple-element.141), channel_id=1, source_target_pairs={{0,16},{1,17},{2,18},{3,19},{4,20},{5,21},{6,22},{7,23},{8,24},{9,... | collective-permute-start | bytes 3145736 | tf_op jit(solution)/shard_map/ppermute | solution.py:283
  135.9 59.5 %collective-permute-start.5 = (bf16[2,16,128,128]{3,2,1,0:T(8,128)(2,1)S(1)}, bf16[2,16,128,128]{3,2,1,0:T(8,128)(2,1)}, u32[]{:S(2)}, u32[]{:S(2)}) collective-permute-start(bf16[2,16,128,128]{3,2,1,0:T(8,128)(2,1)S(1)} %copy-done.8), channel_id=1, source_target_pairs={{0,24},{1,25},{2,26},{3,27},{4,28},{5,29},{6,30},{7,31},{8,16},{9,... | collective-permute-start | bytes 3145736 | tf_op jit(solution)/shard_map/ppermute | solution.py:283
  185.8 27.3 %collective-permute-start.58 = (bf16[2,16,16,128]{3,2,1,0:T(8,128)(2,1)}, bf16[2,16,16,128]{3,2,1,0:T(8,128)(2,1)S(1)}, u32[]{:S(2)}, u32[]{:S(2)}) collective-permute-start(bf16[2,16,16,128]{3,2,1,0:T(8,128)(2,1)} %get-tuple-element.194), channel_id=1, source_target_pairs={{0,7},{1,6},{2,5},{3,4},{4,3},{5,2},{6,1},{7,0},{8,15},{9,14},{10,... | collective-permute-start | bytes 393224 | tf_op jit(solution)/shard_map/ppermute | solution.py:293
  192.1 22.2 %collective-permute-start.60 = (bf16[2,16,16,128]{3,2,1,0:T(8,128)(2,1)}, bf16[2,16,16,128]{3,2,1,0:T(8,128)(2,1)S(1)}, u32[]{:S(2)}, u32[]{:S(2)}) collective-permute-start(bf16[2,16,16,128]{3,2,1,0:T(8,128)(2,1)} %get-tuple-element.196), channel_id=1, source_target_pairs={{0,16},{1,17},{2,18},{3,19},{4,20},{5,21},{6,22},{7,23},{8,24},{9,... | collective-permute-start | bytes 393224 | tf_op jit(solution)/shard_map/ppermute | solution.py:293
  193.4 24.1 %collective-permute-start.62 = (bf16[2,16,16,128]{3,2,1,0:T(8,128)(2,1)}, bf16[2,16,16,128]{3,2,1,0:T(8,128)(2,1)S(1)}, u32[]{:S(2)}, u32[]{:S(2)}) collective-permute-start(bf16[2,16,16,128]{3,2,1,0:T(8,128)(2,1)} %get-tuple-element.198), channel_id=1, source_target_pairs={{0,17},{1,16},{2,19},{3,18},{4,21},{5,20},{6,23},{7,22},{8,25},{9,... | collective-permute-start | bytes 393224 | tf_op jit(solution)/shard_map/ppermute | solution.py:293
  193.4 25.4 %collective-permute-start.64 = (bf16[2,16,16,128]{3,2,1,0:T(8,128)(2,1)}, bf16[2,16,16,128]{3,2,1,0:T(8,128)(2,1)S(1)}, u32[]{:S(2)}, u32[]{:S(2)}) collective-permute-start(bf16[2,16,16,128]{3,2,1,0:T(8,128)(2,1)} %get-tuple-element.200), channel_id=1, source_target_pairs={{0,18},{1,19},{2,16},{3,17},{4,22},{5,23},{6,20},{7,21},{8,26},{9,... | collective-permute-start | bytes 393224 | tf_op jit(solution)/shard_map/ppermute | solution.py:293
  195.4 27.3 %collective-permute-start.66 = (bf16[2,16,16,128]{3,2,1,0:T(8,128)(2,1)}, bf16[2,16,16,128]{3,2,1,0:T(8,128)(2,1)S(1)}, u32[]{:S(2)}, u32[]{:S(2)}) collective-permute-start(bf16[2,16,16,128]{3,2,1,0:T(8,128)(2,1)} %get-tuple-element.202), channel_id=1, source_target_pairs={{0,19},{1,18},{2,17},{3,16},{4,23},{5,22},{6,21},{7,20},{8,27},{9,... | collective-permute-start | bytes 393224 | tf_op jit(solution)/shard_map/ppermute | solution.py:293
  213.0 19.4 %collective-permute-start.68 = (bf16[2,16,16,128]{3,2,1,0:T(8,128)(2,1)S(1)}, bf16[2,16,16,128]{3,2,1,0:T(8,128)(2,1)S(1)}, u32[]{:S(2)}, u32[]{:S(2)}) collective-permute-start(bf16[2,16,16,128]{3,2,1,0:T(8,128)(2,1)S(1)} %copy-done.45), channel_id=1, source_target_pairs={{0,20},{1,21},{2,22},{3,23},{4,16},{5,17},{6,18},{7,19},{8,28},{9,... | collective-permute-start | bytes 393224 | tf_op jit(solution)/shard_map/ppermute | solution.py:293
  214.3 20.4 %collective-permute-start.70 = (bf16[2,16,16,128]{3,2,1,0:T(8,128)(2,1)S(1)}, bf16[2,16,16,128]{3,2,1,0:T(8,128)(2,1)S(1)}, u32[]{:S(2)}, u32[]{:S(2)}) collective-permute-start(bf16[2,16,16,128]{3,2,1,0:T(8,128)(2,1)S(1)} %copy-done.43), channel_id=1, source_target_pairs={{0,21},{1,20},{2,23},{3,22},{4,17},{5,16},{6,19},{7,18},{8,29},{9,... | collective-permute-start | bytes 393224 | tf_op jit(solution)/shard_map/ppermute | solution.py:293
  218.8 19.4 %collective-permute-start.74 = (bf16[2,16,16,128]{3,2,1,0:T(8,128)(2,1)S(1)}, bf16[2,16,16,128]{3,2,1,0:T(8,128)(2,1)S(1)}, u32[]{:S(2)}, u32[]{:S(2)}) collective-permute-start(bf16[2,16,16,128]{3,2,1,0:T(8,128)(2,1)S(1)} %copy-done.40), channel_id=1, source_target_pairs={{0,23},{1,22},{2,21},{3,20},{4,19},{5,18},{6,17},{7,16},{8,31},{9,... | collective-permute-start | bytes 393224 | tf_op jit(solution)/shard_map/ppermute | solution.py:293
  222.8 20.8 %collective-permute-start.7 = (bf16[2,16,16,128]{3,2,1,0:T(8,128)(2,1)}, bf16[2,16,16,128]{3,2,1,0:T(8,128)(2,1)S(1)}, u32[]{:S(2)}, u32[]{:S(2)}) collective-permute-start(bf16[2,16,16,128]{3,2,1,0:T(8,128)(2,1)} %get-tuple-element.145), channel_id=1, source_target_pairs={{0,1},{1,0},{2,3},{3,2},{4,5},{5,4},{6,7},{7,6},{8,9},{9,8},{10,11... | collective-permute-start | bytes 393224 | tf_op jit(solution)/shard_map/ppermute | solution.py:293
  255.5 20.0 %collective-permute-start.55 = (bf16[2,16,16,128]{3,2,1,0:T(8,128)(2,1)}, bf16[2,16,16,128]{3,2,1,0:T(8,128)(2,1)S(1)}, u32[]{:S(2)}, u32[]{:S(2)}) collective-permute-start(bf16[2,16,16,128]{3,2,1,0:T(8,128)(2,1)} %get-tuple-element.191), channel_id=1, source_target_pairs={{0,5},{1,4},{2,7},{3,6},{4,1},{5,0},{6,3},{7,2},{8,13},{9,12},{10,... | collective-permute-start | bytes 393224 | tf_op jit(solution)/shard_map/ppermute | solution.py:293
  278.6 22.6 %collective-permute-start.69 = (bf16[2,16,16,128]{3,2,1,0:T(8,128)(2,1)}, bf16[2,16,16,128]{3,2,1,0:T(8,128)(2,1)S(1)}, u32[]{:S(2)}, u32[]{:S(2)}) collective-permute-start(bf16[2,16,16,128]{3,2,1,0:T(8,128)(2,1)} %get-tuple-element.205), channel_id=1, source_target_pairs={{0,20},{1,21},{2,22},{3,23},{4,16},{5,17},{6,18},{7,19},{8,28},{9,... | collective-permute-start | bytes 393224 | tf_op jit(solution)/shard_map/ppermute | solution.py:293
  282.8 21.3 %collective-permute-start.71 = (bf16[2,16,16,128]{3,2,1,0:T(8,128)(2,1)}, bf16[2,16,16,128]{3,2,1,0:T(8,128)(2,1)S(1)}, u32[]{:S(2)}, u32[]{:S(2)}) collective-permute-start(bf16[2,16,16,128]{3,2,1,0:T(8,128)(2,1)} %get-tuple-element.207), channel_id=1, source_target_pairs={{0,21},{1,20},{2,23},{3,22},{4,17},{5,16},{6,19},{7,18},{8,29},{9,... | collective-permute-start | bytes 393224 | tf_op jit(solution)/shard_map/ppermute | solution.py:293
  292.4 29.4 %collective-permute-start.19 = (bf16[2,16,16,128]{3,2,1,0:T(8,128)(2,1)}, bf16[2,16,16,128]{3,2,1,0:T(8,128)(2,1)S(1)}, u32[]{:S(2)}, u32[]{:S(2)}) collective-permute-start(bf16[2,16,16,128]{3,2,1,0:T(8,128)(2,1)} %get-tuple-element.157), channel_id=1, source_target_pairs={{0,7},{1,6},{2,5},{3,4},{4,3},{5,2},{6,1},{7,0},{8,15},{9,14},{10,... | collective-permute-start | bytes 393224 | tf_op jit(solution)/shard_map/ppermute | solution.py:293
  301.2 22.9 %collective-permute-start.21 = (bf16[2,16,16,128]{3,2,1,0:T(8,128)(2,1)}, bf16[2,16,16,128]{3,2,1,0:T(8,128)(2,1)S(1)}, u32[]{:S(2)}, u32[]{:S(2)}) collective-permute-start(bf16[2,16,16,128]{3,2,1,0:T(8,128)(2,1)} %get-tuple-element.159), channel_id=1, source_target_pairs={{0,16},{1,17},{2,18},{3,19},{4,20},{5,21},{6,22},{7,23},{8,24},{9,... | collective-permute-start | bytes 393224 | tf_op jit(solution)/shard_map/ppermute | solution.py:293
  304.0 23.1 %collective-permute-start.23 = (bf16[2,16,16,128]{3,2,1,0:T(8,128)(2,1)}, bf16[2,16,16,128]{3,2,1,0:T(8,128)(2,1)S(1)}, u32[]{:S(2)}, u32[]{:S(2)}) collective-permute-start(bf16[2,16,16,128]{3,2,1,0:T(8,128)(2,1)} %get-tuple-element.161), channel_id=1, source_target_pairs={{0,17},{1,16},{2,19},{3,18},{4,21},{5,20},{6,23},{7,22},{8,25},{9,... | collective-permute-start | bytes 393224 | tf_op jit(solution)/shard_map/ppermute | solution.py:293
  304.6 25.0 %collective-permute-start.25 = (bf16[2,16,16,128]{3,2,1,0:T(8,128)(2,1)}, bf16[2,16,16,128]{3,2,1,0:T(8,128)(2,1)S(1)}, u32[]{:S(2)}, u32[]{:S(2)}) collective-permute-start(bf16[2,16,16,128]{3,2,1,0:T(8,128)(2,1)} %get-tuple-element.163), channel_id=1, source_target_pairs={{0,18},{1,19},{2,16},{3,17},{4,22},{5,23},{6,20},{7,21},{8,26},{9,... | collective-permute-start | bytes 393224 | tf_op jit(solution)/shard_map/ppermute | solution.py:293
  306.6 24.9 %collective-permute-start.27 = (bf16[2,16,16,128]{3,2,1,0:T(8,128)(2,1)}, bf16[2,16,16,128]{3,2,1,0:T(8,128)(2,1)S(1)}, u32[]{:S(2)}, u32[]{:S(2)}) collective-permute-start(bf16[2,16,16,128]{3,2,1,0:T(8,128)(2,1)} %get-tuple-element.165), channel_id=1, source_target_pairs={{0,19},{1,18},{2,17},{3,16},{4,23},{5,22},{6,21},{7,20},{8,27},{9,... | collective-permute-start | bytes 393224 | tf_op jit(solution)/shard_map/ppermute | solution.py:293
  324.1 19.1 %collective-permute-start.31 = (bf16[2,16,16,128]{3,2,1,0:T(8,128)(2,1)S(1)}, bf16[2,16,16,128]{3,2,1,0:T(8,128)(2,1)S(1)}, u32[]{:S(2)}, u32[]{:S(2)}) collective-permute-start(bf16[2,16,16,128]{3,2,1,0:T(8,128)(2,1)S(1)} %copy-done.50), channel_id=1, source_target_pairs={{0,21},{1,20},{2,23},{3,22},{4,17},{5,16},{6,19},{7,18},{8,29},{9,... | collective-permute-start | bytes 393224 | tf_op jit(solution)/shard_map/ppermute | solution.py:293
  331.6 34.4 %collective-permute-start.76 = (bf16[2,16,256,128]{3,2,1,0:T(8,128)(2,1)}, bf16[2,16,256,128]{3,2,1,0:T(8,128)(2,1)}, u32[]{:S(2)}, u32[]{:S(2)}) collective-permute-start(bf16[2,16,256,128]{3,2,1,0:T(8,128)(2,1)} %get-tuple-element.213), channel_id=1, source_target_pairs={{0,8},{1,9},{2,10},{3,11},{4,12},{5,13},{6,14},{7,15},{8,0},{9,1},... | collective-permute-start | bytes 6291464 | tf_op jit(solution)/shard_map/ppermute | solution.py:283
  356.2 26.0 %collective-permute-start.36 = (bf16[2,16,256,128]{3,2,1,0:T(8,128)(2,1)}, bf16[2,16,256,128]{3,2,1,0:T(8,128)(2,1)}, u32[]{:S(2)}, u32[]{:S(2)}) collective-permute-start(bf16[2,16,256,128]{3,2,1,0:T(8,128)(2,1)} %get-tuple-element.175), channel_id=1, source_target_pairs={{0,8},{1,9},{2,10},{3,11},{4,12},{5,13},{6,14},{7,15},{8,0},{9,1},... | collective-permute-start | bytes 6291464 | tf_op jit(solution)/shard_map/ppermute | solution.py:283
  398.0 23.4 %collective-permute-start.45 = (bf16[2,16,256,128]{3,2,1,0:T(8,128)(2,1)}, bf16[2,16,256,128]{3,2,1,0:T(8,128)(2,1)}, u32[]{:S(2)}, u32[]{:S(2)}) collective-permute-start(bf16[2,16,256,128]{3,2,1,0:T(8,128)(2,1)} %get-tuple-element.178), channel_id=1, source_target_pairs={{0,8},{1,9},{2,10},{3,11},{4,12},{5,13},{6,14},{7,15},{8,0},{9,1},... | collective-permute-start | bytes 6291464 | tf_op jit(solution)/shard_map/ppermute | solution.py:283
  416.3 20.1 %collective-permute-start.81 = (bf16[2,32,16,128]{3,2,1,0:T(8,128)(2,1)}, bf16[2,32,16,128]{3,2,1,0:T(8,128)(2,1)S(1)}, u32[]{:S(2)}, u32[]{:S(2)}) collective-permute-start(bf16[2,32,16,128]{3,2,1,0:T(8,128)(2,1)} %get-tuple-element.220), channel_id=1, source_target_pairs={{0,2},{1,3},{2,0},{3,1},{4,6},{5,7},{6,4},{7,5},{8,10},{9,11},{10,... | collective-permute-start | bytes 786440 | tf_op jit(solution)/shard_map/ppermute | solution.py:293
  420.6 20.9 %collective-permute-start.83 = (bf16[2,32,16,128]{3,2,1,0:T(8,128)(2,1)}, bf16[2,32,16,128]{3,2,1,0:T(8,128)(2,1)S(1)}, u32[]{:S(2)}, u32[]{:S(2)}) collective-permute-start(bf16[2,32,16,128]{3,2,1,0:T(8,128)(2,1)} %get-tuple-element.222), channel_id=1, source_target_pairs={{0,3},{1,2},{2,1},{3,0},{4,7},{5,6},{6,5},{7,4},{8,11},{9,10},{10,... | collective-permute-start | bytes 786440 | tf_op jit(solution)/shard_map/ppermute | solution.py:293
  420.9 21.5 %collective-permute-start.85 = (bf16[2,32,16,128]{3,2,1,0:T(8,128)(2,1)}, bf16[2,32,16,128]{3,2,1,0:T(8,128)(2,1)S(1)}, u32[]{:S(2)}, u32[]{:S(2)}) collective-permute-start(bf16[2,32,16,128]{3,2,1,0:T(8,128)(2,1)} %get-tuple-element.224), channel_id=1, source_target_pairs={{0,4},{1,5},{2,6},{3,7},{4,0},{5,1},{6,2},{7,3},{8,12},{9,13},{10,... | collective-permute-start | bytes 786440 | tf_op jit(solution)/shard_map/ppermute | solution.py:293
  421.4 42.2 %collective-permute-start.87 = (bf16[2,32,16,128]{3,2,1,0:T(8,128)(2,1)}, bf16[2,32,16,128]{3,2,1,0:T(8,128)(2,1)S(1)}, u32[]{:S(2)}, u32[]{:S(2)}) collective-permute-start(bf16[2,32,16,128]{3,2,1,0:T(8,128)(2,1)} %get-tuple-element.226), channel_id=1, source_target_pairs={{0,5},{1,4},{2,7},{3,6},{4,1},{5,0},{6,3},{7,2},{8,13},{9,12},{10,... | collective-permute-start | bytes 786440 | tf_op jit(solution)/shard_map/ppermute | solution.py:293
  424.4 39.2 %collective-permute-start.89 = (bf16[2,32,16,128]{3,2,1,0:T(8,128)(2,1)}, bf16[2,32,16,128]{3,2,1,0:T(8,128)(2,1)S(1)}, u32[]{:S(2)}, u32[]{:S(2)}) collective-permute-start(bf16[2,32,16,128]{3,2,1,0:T(8,128)(2,1)} %get-tuple-element.228), channel_id=1, source_target_pairs={{0,6},{1,7},{2,4},{3,5},{4,2},{5,3},{6,0},{7,1},{8,14},{9,15},{10,... | collective-permute-start | bytes 786440 | tf_op jit(solution)/shard_map/ppermute | solution.py:293
  436.4 33.2 %collective-permute-start.91 = (bf16[2,32,16,128]{3,2,1,0:T(8,128)(2,1)}, bf16[2,32,16,128]{3,2,1,0:T(8,128)(2,1)S(1)}, u32[]{:S(2)}, u32[]{:S(2)}) collective-permute-start(bf16[2,32,16,128]{3,2,1,0:T(8,128)(2,1)} %get-tuple-element.230), channel_id=1, source_target_pairs={{0,7},{1,6},{2,5},{3,4},{4,3},{5,2},{6,1},{7,0},{8,15},{9,14},{10,... | collective-permute-start | bytes 786440 | tf_op jit(solution)/shard_map/ppermute | solution.py:293
  441.4 34.4 %collective-permute-start.93 = (bf16[2,32,16,128]{3,2,1,0:T(8,128)(2,1)}, bf16[2,32,16,128]{3,2,1,0:T(8,128)(2,1)S(1)}, u32[]{:S(2)}, u32[]{:S(2)}) collective-permute-start(bf16[2,32,16,128]{3,2,1,0:T(8,128)(2,1)} %get-tuple-element.232), channel_id=1, source_target_pairs={{0,16},{1,17},{2,18},{3,19},{4,20},{5,21},{6,22},{7,23},{8,24},{9,... | collective-permute-start | bytes 786440 | tf_op jit(solution)/shard_map/ppermute | solution.py:293
  442.4 33.8 %collective-permute-start.95 = (bf16[2,32,16,128]{3,2,1,0:T(8,128)(2,1)}, bf16[2,32,16,128]{3,2,1,0:T(8,128)(2,1)S(1)}, u32[]{:S(2)}, u32[]{:S(2)}) collective-permute-start(bf16[2,32,16,128]{3,2,1,0:T(8,128)(2,1)} %get-tuple-element.234), channel_id=1, source_target_pairs={{0,17},{1,16},{2,19},{3,18},{4,21},{5,20},{6,23},{7,22},{8,25},{9,... | collective-permute-start | bytes 786440 | tf_op jit(solution)/shard_map/ppermute | solution.py:293
  463.6 31.9 %collective-permute-start.99 = (bf16[2,32,16,128]{3,2,1,0:T(8,128)(2,1)}, bf16[2,32,16,128]{3,2,1,0:T(8,128)(2,1)S(1)}, u32[]{:S(2)}, u32[]{:S(2)}) collective-permute-start(bf16[2,32,16,128]{3,2,1,0:T(8,128)(2,1)} %get-tuple-element.238), channel_id=1, source_target_pairs={{0,19},{1,18},{2,17},{3,16},{4,23},{5,22},{6,21},{7,20},{8,27},{9,... | collective-permute-start | bytes 786440 | tf_op jit(solution)/shard_map/ppermute | solution.py:293
  469.6 35.9 %collective-permute-start.101 = (bf16[2,32,16,128]{3,2,1,0:T(8,128)(2,1)}, bf16[2,32,16,128]{3,2,1,0:T(8,128)(2,1)}, u32[]{:S(2)}, u32[]{:S(2)}) collective-permute-start(bf16[2,32,16,128]{3,2,1,0:T(8,128)(2,1)} %get-tuple-element.240), channel_id=1, source_target_pairs={{0,20},{1,21},{2,22},{3,23},{4,16},{5,17},{6,18},{7,19},{8,28},{9,... | collective-permute-start | bytes 786440 | tf_op jit(solution)/shard_map/ppermute | solution.py:293
  475.8 35.3 %collective-permute-start.103 = (bf16[2,32,16,128]{3,2,1,0:T(8,128)(2,1)}, bf16[2,32,16,128]{3,2,1,0:T(8,128)(2,1)}, u32[]{:S(2)}, u32[]{:S(2)}) collective-permute-start(bf16[2,32,16,128]{3,2,1,0:T(8,128)(2,1)} %get-tuple-element.242), channel_id=1, source_target_pairs={{0,21},{1,20},{2,23},{3,22},{4,17},{5,16},{6,19},{7,18},{8,29},{9,... | collective-permute-start | bytes 786440 | tf_op jit(solution)/shard_map/ppermute | solution.py:293
  476.2 34.9 %collective-permute-start.105 = (bf16[2,32,16,128]{3,2,1,0:T(8,128)(2,1)}, bf16[2,32,16,128]{3,2,1,0:T(8,128)(2,1)}, u32[]{:S(2)}, u32[]{:S(2)}) collective-permute-start(bf16[2,32,16,128]{3,2,1,0:T(8,128)(2,1)} %get-tuple-element.244), channel_id=1, source_target_pairs={{0,22},{1,23},{2,20},{3,21},{4,18},{5,19},{6,16},{7,17},{8,30},{9,... | collective-permute-start | bytes 786440 | tf_op jit(solution)/shard_map/ppermute | solution.py:293
  480.6 37.8 %collective-permute-start.107 = (bf16[2,32,16,128]{3,2,1,0:T(8,128)(2,1)}, bf16[2,32,16,128]{3,2,1,0:T(8,128)(2,1)}, u32[]{:S(2)}, u32[]{:S(2)}) collective-permute-start(bf16[2,32,16,128]{3,2,1,0:T(8,128)(2,1)} %get-tuple-element.246), channel_id=1, source_target_pairs={{0,23},{1,22},{2,21},{3,20},{4,19},{5,18},{6,17},{7,16},{8,31},{9,... | collective-permute-start | bytes 786440 | tf_op jit(solution)/shard_map/ppermute | solution.py:293
  496.3 39.8 %collective-permute-start.78 = (bf16[2,32,16,128]{3,2,1,0:T(8,128)(2,1)}, bf16[2,32,16,128]{3,2,1,0:T(8,128)(2,1)S(1)}, u32[]{:S(2)}, u32[]{:S(2)}) collective-permute-start(bf16[2,32,16,128]{3,2,1,0:T(8,128)(2,1)} %get-tuple-element.217), channel_id=1, source_target_pairs={{0,1},{1,0},{2,3},{3,2},{4,5},{5,4},{6,7},{7,6},{8,9},{9,8},{10,11... | collective-permute-start | bytes 786440 | tf_op jit(solution)/shard_map/ppermute | solution.py:293
  505.4 32.9 %collective-permute-start.80 = (bf16[2,32,16,128]{3,2,1,0:T(8,128)(2,1)}, bf16[2,32,16,128]{3,2,1,0:T(8,128)(2,1)S(1)}, u32[]{:S(2)}, u32[]{:S(2)}) collective-permute-start(bf16[2,32,16,128]{3,2,1,0:T(8,128)(2,1)} %get-tuple-element.219), channel_id=1, source_target_pairs={{0,2},{1,3},{2,0},{3,1},{4,6},{5,7},{6,4},{7,5},{8,10},{9,11},{10,... | collective-permute-start | bytes 786440 | tf_op jit(solution)/shard_map/ppermute | solution.py:293
  511.1 29.7 %collective-permute-start.82 = (bf16[2,32,16,128]{3,2,1,0:T(8,128)(2,1)}, bf16[2,32,16,128]{3,2,1,0:T(8,128)(2,1)S(1)}, u32[]{:S(2)}, u32[]{:S(2)}) collective-permute-start(bf16[2,32,16,128]{3,2,1,0:T(8,128)(2,1)} %get-tuple-element.221), channel_id=1, source_target_pairs={{0,3},{1,2},{2,1},{3,0},{4,7},{5,6},{6,5},{7,4},{8,11},{9,10},{10,... | collective-permute-start | bytes 786440 | tf_op jit(solution)/shard_map/ppermute | solution.py:293
  511.1 39.6 %collective-permute-start.84 = (bf16[2,32,16,128]{3,2,1,0:T(8,128)(2,1)}, bf16[2,32,16,128]{3,2,1,0:T(8,128)(2,1)S(1)}, u32[]{:S(2)}, u32[]{:S(2)}) collective-permute-start(bf16[2,32,16,128]{3,2,1,0:T(8,128)(2,1)} %get-tuple-element.223), channel_id=1, source_target_pairs={{0,4},{1,5},{2,6},{3,7},{4,0},{5,1},{6,2},{7,3},{8,12},{9,13},{10,... | collective-permute-start | bytes 786440 | tf_op jit(solution)/shard_map/ppermute | solution.py:293
  518.4 38.0 %collective-permute-start.86 = (bf16[2,32,16,128]{3,2,1,0:T(8,128)(2,1)}, bf16[2,32,16,128]{3,2,1,0:T(8,128)(2,1)S(1)}, u32[]{:S(2)}, u32[]{:S(2)}) collective-permute-start(bf16[2,32,16,128]{3,2,1,0:T(8,128)(2,1)} %get-tuple-element.225), channel_id=1, source_target_pairs={{0,5},{1,4},{2,7},{3,6},{4,1},{5,0},{6,3},{7,2},{8,13},{9,12},{10,... | collective-permute-start | bytes 786440 | tf_op jit(solution)/shard_map/ppermute | solution.py:293
  536.1 20.4 %collective-permute-start.88 = (bf16[2,32,16,128]{3,2,1,0:T(8,128)(2,1)}, bf16[2,32,16,128]{3,2,1,0:T(8,128)(2,1)}, u32[]{:S(2)}, u32[]{:S(2)}) collective-permute-start(bf16[2,32,16,128]{3,2,1,0:T(8,128)(2,1)} %get-tuple-element.227), channel_id=1, source_target_pairs={{0,6},{1,7},{2,4},{3,5},{4,2},{5,3},{6,0},{7,1},{8,14},{9,15},{10,... | collective-permute-start | bytes 786440 | tf_op jit(solution)/shard_map/ppermute | solution.py:293
  538.3 24.0 %collective-permute-start.90 = (bf16[2,32,16,128]{3,2,1,0:T(8,128)(2,1)}, bf16[2,32,16,128]{3,2,1,0:T(8,128)(2,1)}, u32[]{:S(2)}, u32[]{:S(2)}) collective-permute-start(bf16[2,32,16,128]{3,2,1,0:T(8,128)(2,1)} %get-tuple-element.229), channel_id=1, source_target_pairs={{0,7},{1,6},{2,5},{3,4},{4,3},{5,2},{6,1},{7,0},{8,15},{9,14},{10,... | collective-permute-start | bytes 786440 | tf_op jit(solution)/shard_map/ppermute | solution.py:293
  540.9 27.7 %collective-permute-start.92 = (bf16[2,32,16,128]{3,2,1,0:T(8,128)(2,1)}, bf16[2,32,16,128]{3,2,1,0:T(8,128)(2,1)}, u32[]{:S(2)}, u32[]{:S(2)}) collective-permute-start(bf16[2,32,16,128]{3,2,1,0:T(8,128)(2,1)} %get-tuple-element.231), channel_id=1, source_target_pairs={{0,16},{1,17},{2,18},{3,19},{4,20},{5,21},{6,22},{7,23},{8,24},{9,... | collective-permute-start | bytes 786440 | tf_op jit(solution)/shard_map/ppermute | solution.py:293
  550.7 21.8 %collective-permute-start.94 = (bf16[2,32,16,128]{3,2,1,0:T(8,128)(2,1)}, bf16[2,32,16,128]{3,2,1,0:T(8,128)(2,1)}, u32[]{:S(2)}, u32[]{:S(2)}) collective-permute-start(bf16[2,32,16,128]{3,2,1,0:T(8,128)(2,1)} %get-tuple-element.233), channel_id=1, source_target_pairs={{0,17},{1,16},{2,19},{3,18},{4,21},{5,20},{6,23},{7,22},{8,25},{9,... | collective-permute-start | bytes 786440 | tf_op jit(solution)/shard_map/ppermute | solution.py:293
  556.4 22.8 %collective-permute-start.98 = (bf16[2,32,16,128]{3,2,1,0:T(8,128)(2,1)}, bf16[2,32,16,128]{3,2,1,0:T(8,128)(2,1)}, u32[]{:S(2)}, u32[]{:S(2)}) collective-permute-start(bf16[2,32,16,128]{3,2,1,0:T(8,128)(2,1)} %get-tuple-element.237), channel_id=1, source_target_pairs={{0,19},{1,18},{2,17},{3,16},{4,23},{5,22},{6,21},{7,20},{8,27},{9,... | collective-permute-start | bytes 786440 | tf_op jit(solution)/shard_map/ppermute | solution.py:293
  562.3 35.3 %collective-permute-start.100 = (bf16[2,32,16,128]{3,2,1,0:T(8,128)(2,1)}, bf16[2,32,16,128]{3,2,1,0:T(8,128)(2,1)}, u32[]{:S(2)}, u32[]{:S(2)}) collective-permute-start(bf16[2,32,16,128]{3,2,1,0:T(8,128)(2,1)} %get-tuple-element.239), channel_id=1, source_target_pairs={{0,20},{1,21},{2,22},{3,23},{4,16},{5,17},{6,18},{7,19},{8,28},{9,... | collective-permute-start | bytes 786440 | tf_op jit(solution)/shard_map/ppermute | solution.py:293
  568.6 35.4 %collective-permute-start.102 = (bf16[2,32,16,128]{3,2,1,0:T(8,128)(2,1)}, bf16[2,32,16,128]{3,2,1,0:T(8,128)(2,1)}, u32[]{:S(2)}, u32[]{:S(2)}) collective-permute-start(bf16[2,32,16,128]{3,2,1,0:T(8,128)(2,1)} %get-tuple-element.241), channel_id=1, source_target_pairs={{0,21},{1,20},{2,23},{3,22},{4,17},{5,16},{6,19},{7,18},{8,29},{9,... | collective-permute-start | bytes 786440 | tf_op jit(solution)/shard_map/ppermute | solution.py:293
  572.5 31.5 %collective-permute-start.104 = (bf16[2,32,16,128]{3,2,1,0:T(8,128)(2,1)}, bf16[2,32,16,128]{3,2,1,0:T(8,128)(2,1)}, u32[]{:S(2)}, u32[]{:S(2)}) collective-permute-start(bf16[2,32,16,128]{3,2,1,0:T(8,128)(2,1)} %get-tuple-element.243), channel_id=1, source_target_pairs={{0,22},{1,23},{2,20},{3,21},{4,18},{5,19},{6,16},{7,17},{8,30},{9,... | collective-permute-start | bytes 786440 | tf_op jit(solution)/shard_map/ppermute | solution.py:293
  573.9 30.2 %collective-permute-start.106 = (bf16[2,32,16,128]{3,2,1,0:T(8,128)(2,1)}, bf16[2,32,16,128]{3,2,1,0:T(8,128)(2,1)}, u32[]{:S(2)}, u32[]{:S(2)}) collective-permute-start(bf16[2,32,16,128]{3,2,1,0:T(8,128)(2,1)} %get-tuple-element.245), channel_id=1, source_target_pairs={{0,23},{1,22},{2,21},{3,20},{4,19},{5,18},{6,17},{7,16},{8,31},{9,... | collective-permute-start | bytes 786440 | tf_op jit(solution)/shard_map/ppermute | solution.py:293
  618.5 26.3 %collective-permute-start.111 = (bf16[2,128,16,128]{3,2,1,0:T(8,128)(2,1)}, bf16[2,128,16,128]{3,2,1,0:T(8,128)(2,1)S(1)}, u32[]{:S(2)}, u32[]{:S(2)}) collective-permute-start(bf16[2,128,16,128]{3,2,1,0:T(8,128)(2,1)} %get-tuple-element.251), channel_id=1, source_target_pairs={{0,16},{1,17},{2,18},{3,19},{4,20},{5,21},{6,22},{7,23},{8,24},{9,... | collective-permute-start | bytes 3145736 | tf_op jit(solution)/shard_map/ppermute | solution.py:283
  620.2 46.3 %collective-permute-start.112 = (bf16[2,128,16,128]{3,2,1,0:T(8,128)(2,1)}, bf16[2,128,16,128]{3,2,1,0:T(8,128)(2,1)}, u32[]{:S(2)}, u32[]{:S(2)}) collective-permute-start(bf16[2,128,16,128]{3,2,1,0:T(8,128)(2,1)} %get-tuple-element.252), channel_id=1, source_target_pairs={{0,24},{1,25},{2,26},{3,27},{4,28},{5,29},{6,30},{7,31},{8,16},{9,... | collective-permute-start | bytes 3145736 | tf_op jit(solution)/shard_map/ppermute | solution.py:283
  634.8 36.3 %collective-permute-start.110 = (bf16[2,128,16,128]{3,2,1,0:T(8,128)(2,1)}, bf16[2,128,16,128]{3,2,1,0:T(8,128)(2,1)}, u32[]{:S(2)}, u32[]{:S(2)}) collective-permute-start(bf16[2,128,16,128]{3,2,1,0:T(8,128)(2,1)} %get-tuple-element.250), channel_id=1, source_target_pairs={{0,8},{1,9},{2,10},{3,11},{4,12},{5,13},{6,14},{7,15},{8,0},{9,1},... | collective-permute-start | bytes 3145736 | tf_op jit(solution)/shard_map/ppermute | solution.py:283
  635.2 54.7 %collective-permute-start.108 = (bf16[2,128,16,128]{3,2,1,0:T(8,128)(2,1)}, bf16[2,128,16,128]{3,2,1,0:T(8,128)(2,1)}, u32[]{:S(2)}, u32[]{:S(2)}) collective-permute-start(bf16[2,128,16,128]{3,2,1,0:T(8,128)(2,1)} %get-tuple-element.247), channel_id=1, source_target_pairs={{0,16},{1,17},{2,18},{3,19},{4,20},{5,21},{6,22},{7,23},{8,24},{9,... | collective-permute-start | bytes 3145736 | tf_op jit(solution)/shard_map/ppermute | solution.py:283
  636.8 74.5 %collective-permute-start.109 = (bf16[2,128,16,128]{3,2,1,0:T(8,128)(2,1)}, bf16[2,128,16,128]{3,2,1,0:T(8,128)(2,1)}, u32[]{:S(2)}, u32[]{:S(2)}) collective-permute-start(bf16[2,128,16,128]{3,2,1,0:T(8,128)(2,1)} %get-tuple-element.248), channel_id=1, source_target_pairs={{0,24},{1,25},{2,26},{3,27},{4,28},{5,29},{6,30},{7,31},{8,16},{9,... | collective-permute-start | bytes 3145736 | tf_op jit(solution)/shard_map/ppermute | solution.py:283
  (141 other events, 3929.9 us)
where the time goes:
time: 725 us; the launch traced here: 716 us
  waiting for transfers between devices  251 us (35%)
  starting transfers between devices  234 us (32%)
  Pallas kernels  193 us (27%)
  local copies, waits for them, and re-layouts  14.5 us (2%)
  other arithmetic  12.5 us (2%)
  matrix products  9.22 us (1%)
    ppermute x90, starting transfers between devices, send_far(): return lax.ppermute(piece, axes, pairs)  213 us
    ppermute x90, waiting for transfers between devices, send_far(): return lax.ppermute(piece, axes, pairs)  167 us
    pallas_call x8, Pallas kernels, propagate(): pl.pallas_call(functools.partial(prop_kernel, turned, len(pieces), n_out)...  106 us
    ppermute x16, waiting for transfers between devices, send_near(): lax.ppermute(piece, axes, [(index(i, j), index(i ^ s, j)) for i in range(...  74.4 us
    pallas_call x4, Pallas kernels, kick_turned(): pl.pallas_call(kick_turned_kernel, grid_spec=spec, out_shape=[shape, shap...  37.7 us
    pallas_call x2, Pallas kernels, kick_pair(): pl.pallas_call(kick_pair_kernel, grid=(a_rows,), in_specs=[block, block,...  31.5 us
    pallas_call x4, Pallas kernels, join(): pl.pallas_call(join_kernel, grid_spec=spec, out_shape=jax.ShapeDtypeStruc...  18.2 us
  transfers between devices with their start and end apart: 114, of which 40 were waited for; matrix products, arithmetic and copies ran while one was open for 3% of the time, Pallas kernels for 21%

commit v1 on v0

--- a/solution.py
+++ b/solution.py
@@ -323,7 +323,17 @@
         for s in reversed(range(ra // 2)):
             made[2 * s], made[2 * s + 1] = kick_turned(amplitude, weights, near_radial, block_of(s, part))
         kicks.append(made)
-    later_radial = lax.optimization_barrier((radial, kicks[-1]))[0]
+    halves = []
+    for part in range(b_parts):
+        made = kicks[part]
+        if part:
+            made = lax.optimization_barrier((made, pieces))[0]
+        pieces = [send_near(made[s], s) for s in range(ra)]
+        spread = propagate(first_out, pieces, 0, far, True)
+        halves.append([send_far(h, s) for s, h in enumerate(spread)])
+    gathered = [halves[part][s] for s in range(far) for part in range(b_parts)]
+
+    later_radial = lax.optimization_barrier((radial, spread))[0]
 
     got = []
     for u in range(rb):
@@ -335,20 +345,6 @@
         to = (half * half_rb + at_b % half_rb) ^ u
         piece = lax.dynamic_slice_in_dim(later_radial, to * half_far, half_far, axis=1)
         got.append(lax.ppermute(piece, axes, pairs))
-
-    halves, held = [], []
-    for part in range(b_parts):
-        made = kicks[part]
-        if part:
-            made = lax.optimization_barrier((made, pieces))[0]
-        pieces = [send_near(made[s], s) for s in range(ra)]
-        spread = propagate(first_out, pieces, 0, far * a_parts, True)
-        held.append([spread[p::a_parts] for p in range(a_parts)])
-    for p in range(a_parts):
-        for part in range(b_parts):
-            sent = held[part][p]
-            halves.append([send_far(h, s) for s, h in enumerate(sent)])
-    halves = [halves[p * b_parts:(p + 1) * b_parts] for p in range(a_parts)]
 
     turned = weights.reshape(2, 2, LANES, KTERMS * LANES)
     turned = jnp.where(half == 0, turned, turned[:, ::-1]).reshape(weights.shape)
@@ -361,8 +357,7 @@
     far_radial = ordered.transpose(0, 3, 1, 4, 2).reshape(a_far, half_b, KTERMS)
     back = []
     for part in range(a_parts):
-        gathered = [halves[part][q][s] for s in range(far) for q in range(b_parts)]
-        own, other = propagate(second_in, gathered, 0, 2, False)
+        own, other = propagate(second_in, gathered, part, 2, False)
         other = send_near(other, 1)
         own, other = kick_pair(own, other, turned, far_radial, part)
         other = send_near(other, 1)

time: 725 us -> 716 us (0.988)
  starting transfers between devices: 234 us -> 202 us
  waiting for transfers between devices: 251 us -> 273 us
    ppermute x90 -> x60, starting transfers between devices: 213 us -> 189 us  [send_far(): return lax.ppermute(piece, axes, pairs)]
    ppermute x90 -> x60, waiting for transfers between devices: 167 us -> 190 us  [send_far(): return lax.ppermute(piece, axes, pairs)]
    ppermute x8, waiting for transfers between devices: 9.76 us -> 0.02 us  [on_device(): got.append(lax.ppermute(piece, axes, pairs))]
    ppermute x8, starting transfers between devices: 12.1 us -> 3.06 us  [on_device(): got.append(lax.ppermute(piece, axes, pairs))]
    ppermute x16, waiting for transfers between devices: 74.4 us -> 83 us  [send_near(): lax.ppermute(piece, axes, [(index(i, j), index(i ^ s, j)) for i in range(...]
  transfers between devices with their start and end apart: 114 -> 84, of which waited for: 40 -> 26; matrix products, arithmetic and copies ran while one was open for 3% -> 3% of each run, Pallas kernels for 21% -> 21%
where the time goes in v1:
time: 716 us; the launch traced here: 703 us
  waiting for transfers between devices  273 us (38%)
  starting transfers between devices  202 us (28%)
  Pallas kernels  193 us (27%)
  local copies, waits for them, and re-layouts  13.8 us (2%)
  other arithmetic  12.4 us (2%)
  matrix products  9.18 us (1%)
    ppermute x60, waiting for transfers between devices, send_far(): return lax.ppermute(piece, axes, pairs)  190 us
    ppermute x60, starting transfers between devices, send_far(): return lax.ppermute(piece, axes, pairs)  189 us
    pallas_call x8, Pallas kernels, propagate(): pl.pallas_call(functools.partial(prop_kernel, turned, len(pieces), n_out)...  105 us
    ppermute x16, waiting for transfers between devices, send_near(): lax.ppermute(piece, axes, [(index(i, j), index(i ^ s, j)) for i in range(...  83 us
    pallas_call x4, Pallas kernels, kick_turned(): pl.pallas_call(kick_turned_kernel, grid_spec=spec, out_shape=[shape, shap...  37.8 us
    pallas_call x2, Pallas kernels, kick_pair(): pl.pallas_call(kick_pair_kernel, grid=(a_rows,), in_specs=[block, block,...  31.5 us
    pallas_call x4, Pallas kernels, join(): pl.pallas_call(join_kernel, grid_spec=spec, out_shape=jax.ShapeDtypeStruc...  18.2 us
  transfers between devices with their start and end apart: 84, of which 26 were waited for; matrix products, arithmetic and copies ran while one was open for 3% of the time, Pallas kernels for 21%

profile of v1, /device:TPU:0, one launch (start us, length us, event | category | flops | bytes accessed | tf_op | source)
XLA Modules:
  0.0 703.3 jit_solution(12466950134832521027)
XLA Ops:
  4.7 4.4 copy.32
  10.8 9.4 %shard_map.65 = (bf16[2,16,128,128]{3,2,1,0:T(8,128)(2,1)}, bf16[2,16,128,128]{3,2,1,0:T(8,128)(2,1)}) custom-call(s32[2]{0:T(128)} %get-tuple-element.205.where_ref, bf16[2,128,64,256]{3,2,1,0:T(8,128)(2,1)} %amp_ref.7, bf16[2,256,768]{2,1,0:T(8,128)(2,1)} %reverse_select_fusion.3.weights_ref, f32[128,64,6]{2,1,0:T(8,128)} %bitcast.76), custom_call_target="tpu_custom_call" | custom-call | flops 3221225472 | bytes 4194304 | tf_op jit(solution)/shard_map/pallas_call | solution.py:179
  20.2 3.0 collective-permute-start.1
  23.8 9.5 %shard_map.64 = (bf16[2,16,128,128]{3,2,1,0:T(8,128)(2,1)}, bf16[2,16,128,128]{3,2,1,0:T(8,128)(2,1)}) custom-call(s32[2]{0:T(128)} %get-tuple-element.204.where_ref, bf16[2,128,64,256]{3,2,1,0:T(8,128)(2,1)} %amp_ref.7, bf16[2,256,768]{2,1,0:T(8,128)(2,1)} %reverse_select_fusion.3.weights_ref, f32[128,64,6]{2,1,0:T(8,128)} %bitcast.77), custom_call_target="tpu_custom_call" | custom-call | flops 3221225472 | bytes 4194304 | tf_op jit(solution)/shard_map/pallas_call | solution.py:179
  35.8 9.4 %shard_map.68 = (bf16[2,16,128,128]{3,2,1,0:T(8,128)(2,1)}, bf16[2,16,128,128]{3,2,1,0:T(8,128)(2,1)}) custom-call(s32[2]{0:T(128)} %get-tuple-element.203.where_ref, bf16[2,128,64,256]{3,2,1,0:T(8,128)(2,1)} %amp_ref.7, bf16[2,256,768]{2,1,0:T(8,128)(2,1)} %reverse_select_fusion.3.weights_ref, f32[128,64,6]{2,1,0:T(8,128)} %bitcast.78), custom_call_target="tpu_custom_call" | custom-call | flops 3221225472 | bytes 4194304 | tf_op jit(solution)/shard_map/pallas_call | solution.py:179
  47.3 21.0 %collective-permute-done.2.refs_3_ = bf16[2,16,128,128]{3,2,1,0:T(8,128)(2,1)} collective-permute-done((bf16[2,16,128,128]{3,2,1,0:T(8,128)(2,1)}, bf16[2,16,128,128]{3,2,1,0:T(8,128)(2,1)}, u32[]{:S(2)}, u32[]{:S(2)}) %collective-permute-start.2) | collective-permute-done | bytes 1048608 | tf_op jit(solution)/shard_map/ppermute | solution.py:283
  68.3 13.8 %shard_map.66 = (bf16[2,32,16,128]{3,2,1,0:T(8,128)(2,1)}, bf16[2,32,16,128]{3,2,1,0:T(8,128)(2,1)}, bf16[2,32,16,128]{3,2,1,0:T(8,128)(2,1)}, bf16[2,32,16,128]...) custom-call(bf16[2,512,512]{2,1,0:T(8,128)(2,1)} %convolution_conver, ...), custom_call_target="tpu_custom_call" | custom-call | flops 4294967296 | bytes 8388608 | tf_op jit(solution)/shard_map/pallas_call | solution.py:128
  88.3 9.5 %shard_map.67 = (bf16[2,16,128,128]{3,2,1,0:T(8,128)(2,1)}, bf16[2,16,128,128]{3,2,1,0:T(8,128)(2,1)}) custom-call(s32[2]{0:T(128)} %get-tuple-element.206.where_ref, bf16[2,128,64,256]{3,2,1,0:T(8,128)(2,1)} %amp_ref.7, bf16[2,256,768]{2,1,0:T(8,128)(2,1)} %reverse_select_fusion.3.weights_ref, f32[128,64,6]{2,1,0:T(8,128)} %bitcast.79), custom_call_target="tpu_custom_call" | custom-call | flops 3221225472 | bytes 4194304 | tf_op jit(solution)/shard_map/pallas_call | solution.py:179
  99.7 4.1 collective-permute-done.10.refs_6_
  107.6 18.7 %collective-permute-done.14.refs_10_ = bf16[2,32,16,128]{3,2,1,0:T(8,128)(2,1)} collective-permute-done((bf16[2,32,16,128]{3,2,1,0:T(8,128)(2,1)}, bf16[2,32,16,128]{3,2,1,0:T(8,128)(2,1)}, u32[]{:S(2)}, u32[]{:S(2)}) %collective-permute-start.14) | collective-permute-done | bytes 262176 | tf_op jit(solution)/shard_map/ppermute | solution.py:293
  129.5 6.3 collective-permute-done.18.refs_14_
  135.8 3.3 collective-permute-start.22
  139.1 13.0 %collective-permute-done.20.refs_16_ = bf16[2,32,16,128]{3,2,1,0:T(8,128)(2,1)} collective-permute-done((bf16[2,32,16,128]{3,2,1,0:T(8,128)(2,1)}, bf16[2,32,16,128]{3,2,1,0:T(8,128)(2,1)}, u32[]{:S(2)}, u32[]{:S(2)}) %collective-permute-start.20) | collective-permute-done | bytes 262176 | tf_op jit(solution)/shard_map/ppermute | solution.py:293
  154.5 9.3 %collective-permute-done.22.refs_18_ = bf16[2,32,16,128]{3,2,1,0:T(8,128)(2,1)} collective-permute-done((bf16[2,32,16,128]{3,2,1,0:T(8,128)(2,1)}, bf16[2,32,16,128]{3,2,1,0:T(8,128)(2,1)}, u32[]{:S(2)}, u32[]{:S(2)}) %collective-permute-start.22) | collective-permute-done | bytes 262176 | tf_op jit(solution)/shard_map/ppermute | solution.py:293
  166.5 4.3 collective-permute-start.30
  171.2 4.3 collective-permute-start.34
  175.5 13.8 %shard_map.69 = (bf16[2,32,16,128]{3,2,1,0:T(8,128)(2,1)}, bf16[2,32,16,128]{3,2,1,0:T(8,128)(2,1)}, bf16[2,32,16,128]{3,2,1,0:T(8,128)(2,1)}, bf16[2,32,16,128]...) custom-call(bf16[2,512,512]{2,1,0:T(8,128)(2,1)} %convolution_conver, ...), custom_call_target="tpu_custom_call" | custom-call | flops 4294967296 | bytes 8388608 | tf_op jit(solution)/shard_map/pallas_call | solution.py:128
  189.7 10.4 %collective-permute-done.28.refs_24_ = bf16[2,32,16,128]{3,2,1,0:T(8,128)(2,1)} collective-permute-done((bf16[2,32,16,128]{3,2,1,0:T(8,128)(2,1)}, bf16[2,32,16,128]{3,2,1,0:T(8,128)(2,1)}, u32[]{:S(2)}, u32[]{:S(2)}) %collective-permute-start.28) | collective-permute-done | bytes 262176 | tf_op jit(solution)/shard_map/ppermute | solution.py:293
  200.0 7.1 %collective-permute-done.30.refs_26_ = bf16[2,32,16,128]{3,2,1,0:T(8,128)(2,1)} collective-permute-done((bf16[2,32,16,128]{3,2,1,0:T(8,128)(2,1)}, bf16[2,32,16,128]{3,2,1,0:T(8,128)(2,1)}, u32[]{:S(2)}, u32[]{:S(2)}) %collective-permute-start.30) | collective-permute-done | bytes 262176 | tf_op jit(solution)/shard_map/ppermute | solution.py:293
  212.5 11.0 %collective-permute-start.9 = (bf16[2,32,16,128]{3,2,1,0:T(8,128)(2,1)}, bf16[2,32,16,128]{3,2,1,0:T(8,128)(2,1)S(1)}, u32[]{:S(2)}, u32[]{:S(2)}) collective-permute-start(bf16[2,32,16,128]{3,2,1,0:T(8,128)(2,1)} %get-tuple-element.115), channel_id=1, source_target_pairs={{0,2},{1,3},{2,0},{3,1},{4,6},{5,7},{6,4},{7,5},{8,10},{9,11},{10,... | collective-permute-start | bytes 786440 | tf_op jit(solution)/shard_map/ppermute | solution.py:293
  228.5 3.2 collective-permute-start.17
  231.6 10.9 %collective-permute-start.19 = (bf16[2,32,16,128]{3,2,1,0:T(8,128)(2,1)}, bf16[2,32,16,128]{3,2,1,0:T(8,128)(2,1)S(1)}, u32[]{:S(2)}, u32[]{:S(2)}) collective-permute-start(bf16[2,32,16,128]{3,2,1,0:T(8,128)(2,1)} %get-tuple-element.125), channel_id=1, source_target_pairs={{0,7},{1,6},{2,5},{3,4},{4,3},{5,2},{6,1},{7,0},{8,15},{9,14},{10,... | collective-permute-start | bytes 786440 | tf_op jit(solution)/shard_map/ppermute | solution.py:293
  243.1 13.6 %collective-permute-done.13.refs_9_ = bf16[2,32,16,128]{3,2,1,0:T(8,128)(2,1)} collective-permute-done((bf16[2,32,16,128]{3,2,1,0:T(8,128)(2,1)}, bf16[2,32,16,128]{3,2,1,0:T(8,128)(2,1)}, u32[]{:S(2)}, u32[]{:S(2)}) %collective-permute-start.13) | collective-permute-done | bytes 262176 | tf_op jit(solution)/shard_map/ppermute | solution.py:293
  256.7 6.5 collective-permute-done.15.refs_11_
  263.2 4.9 collective-permute-start.27
  268.1 6.6 collective-permute-start.29
  278.8 10.8 %collective-permute-start.35 = (bf16[2,32,16,128]{3,2,1,0:T(8,128)(2,1)S(1)}, bf16[2,32,16,128]{3,2,1,0:T(8,128)(2,1)S(1)}, u32[]{:S(2)}, u32[]{:S(2)}) collective-permute-start(bf16[2,32,16,128]{3,2,1,0:T(8,128)(2,1)S(1)} %copy-done.13), channel_id=1, source_target_pairs={{0,23},{1,22},{2,21},{3,20},{4,19},{5,18},{6,17},{7,16},{8,31},{9,... | collective-permute-start | bytes 786440 | tf_op jit(solution)/shard_map/ppermute | solution.py:293
  289.7 15.3 %collective-permute-done.29.refs_25_ = bf16[2,32,16,128]{3,2,1,0:T(8,128)(2,1)S(1)} collective-permute-done((bf16[2,32,16,128]{3,2,1,0:T(8,128)(2,1)}, bf16[2,32,16,128]{3,2,1,0:T(8,128)(2,1)S(1)}, u32[]{:S(2)}, u32[]{:S(2)}) %collective-permute-start.29) | collective-permute-done | bytes 262176 | tf_op jit(solution)/shard_map/ppermute | solution.py:293
  306.3 6.2 collective-permute-done.31.refs_27_
  313.6 10.5 %shard_map.73 = (bf16[2,16,256,128]{3,2,1,0:T(8,128)(2,1)}, bf16[2,16,256,128]{3,2,1,0:T(8,128)(2,1)}) custom-call(bf16[2,512,512]{2,1,0:T(8,128)(2,1)} %convolution_convert_fusion.2.mat_ref, bf16[2,32,16,128]{3,2,1,0:T(8,128)(2,1)} %get-tuple-element.102.refs_0_, bf16[2,32,16,128]{3,2,1,0:T(8,128)(2,1)} %get-tuple-element.111.refs_1_, ...), custom_call_target="tpu_custom_call" | custom-call | flops 4294967296 | bytes 8388608 | tf_op jit(solution)/shard_map/pallas_call | solution.py:128
  324.2 10.6 %shard_map.70 = (bf16[2,16,256,128]{3,2,1,0:T(8,128)(2,1)}, bf16[2,16,256,128]{3,2,1,0:T(8,128)(2,1)}) custom-call(bf16[2,512,512]{2,1,0:T(8,128)(2,1)} %convolution_convert_fusion.2.mat_ref, bf16[2,32,16,128]{3,2,1,0:T(8,128)(2,1)} %get-tuple-element.102.refs_0_, bf16[2,32,16,128]{3,2,1,0:T(8,128)(2,1)} %get-tuple-element.111.refs_1_, ...), custom_call_target="tpu_custom_call" | custom-call | flops 4294967296 | bytes 8388608 | tf_op jit(solution)/shard_map/pallas_call | solution.py:128
  338.1 4.4 reverse_select_fusion.1
  345.0 15.8 %shard_map.74 = (bf16[2,16,256,128]{3,2,1,0:T(8,128)(2,1)}, bf16[2,16,256,128]{3,2,1,0:T(8,128)(2,1)}) custom-call(bf16[2,16,256,128]{3,2,1,0:T(8,128)(2,1)} %get-tuple-element.148.own_ref, bf16[2,16,256,128]{3,2,1,0:T(8,128)(2,1)} %collective-permute-done.46.other_ref, bf16[2,256,768]{2,1,0:T(8,128)(2,1)} %bitcast.87, f32[32,256,6]{2,1,0:T(8,128)} %bitcast.82), custom_call_target="tpu_custom_call" | custom-call | flops 6442450944 | bytes 8388608 | tf_op jit(solution)/shard_map/pallas_call | solution.py:204
  362.1 15.7 %shard_map.71 = (bf16[2,16,256,128]{3,2,1,0:T(8,128)(2,1)}, bf16[2,16,256,128]{3,2,1,0:T(8,128)(2,1)}) custom-call(bf16[2,16,256,128]{3,2,1,0:T(8,128)(2,1)} %get-tuple-element.142.own_ref, bf16[2,16,256,128]{3,2,1,0:T(8,128)(2,1)} %copy-done.5, bf16[2,256,768]{2,1,0:T(8,128)(2,1)} %bitcast.88, f32[32,256,6]{2,1,0:T(8,128)} %bitcast.83), custom_call_target="tpu_custom_call" | custom-call | flops 6442450944 | bytes 8388608 | tf_op jit(solution)/shard_map/pallas_call | solution.py:204
  380.6 13.7 %shard_map.75 = (bf16[2,32,16,128]{3,2,1,0:T(8,128)(2,1)}, bf16[2,32,16,128]{3,2,1,0:T(8,128)(2,1)}, bf16[2,32,16,128]{3,2,1,0:T(8,128)(2,1)}, bf16[2,32,16,128]...) custom-call(bf16[2,512,512]{2,1,0:T(8,128)(2,1)} %convolution_conver, ...), custom_call_target="tpu_custom_call" | custom-call | flops 4294967296 | bytes 8388608 | tf_op jit(solution)/shard_map/pallas_call | solution.py:128
  395.7 10.8 %collective-permute-start.51 = (bf16[2,32,16,128]{3,2,1,0:T(8,128)(2,1)}, bf16[2,32,16,128]{3,2,1,0:T(8,128)(2,1)S(1)}, u32[]{:S(2)}, u32[]{:S(2)}) collective-permute-start(bf16[2,32,16,128]{3,2,1,0:T(8,128)(2,1)} %get-tuple-element.156), channel_id=1, source_target_pairs={{0,2},{1,3},{2,0},{3,1},{4,6},{5,7},{6,4},{7,5},{8,10},{9,11},{10,... | collective-permute-start | bytes 786440 | tf_op jit(solution)/shard_map/ppermute | solution.py:293
  412.0 11.7 %collective-permute-done.51.refs_5_ = bf16[2,32,16,128]{3,2,1,0:T(8,128)(2,1)S(1)} collective-permute-done((bf16[2,32,16,128]{3,2,1,0:T(8,128)(2,1)}, bf16[2,32,16,128]{3,2,1,0:T(8,128)(2,1)S(1)}, u32[]{:S(2)}, u32[]{:S(2)}) %collective-permute-start.51) | collective-permute-done | bytes 262176 | tf_op jit(solution)/shard_map/ppermute | solution.py:293
  426.5 2.9 collective-permute-done.53.refs_7_
  431.3 17.1 %collective-permute-done.57.refs_11_ = bf16[2,32,16,128]{3,2,1,0:T(8,128)(2,1)S(1)} collective-permute-done((bf16[2,32,16,128]{3,2,1,0:T(8,128)(2,1)}, bf16[2,32,16,128]{3,2,1,0:T(8,128)(2,1)S(1)}, u32[]{:S(2)}, u32[]{:S(2)}) %collective-permute-start.57) | collective-permute-done | bytes 262176 | tf_op jit(solution)/shard_map/ppermute | solution.py:293
  448.9 6.4 collective-permute-start.69
  455.3 7.7 %collective-permute-start.71 = (bf16[2,32,16,128]{3,2,1,0:T(8,128)(2,1)}, bf16[2,32,16,128]{3,2,1,0:T(8,128)(2,1)}, u32[]{:S(2)}, u32[]{:S(2)}) collective-permute-start(bf16[2,32,16,128]{3,2,1,0:T(8,128)(2,1)} %get-tuple-element.176), channel_id=1, source_target_pairs={{0,20},{1,21},{2,22},{3,23},{4,16},{5,17},{6,18},{7,19},{8,28},{9,... | collective-permute-start | bytes 786440 | tf_op jit(solution)/shard_map/ppermute | solution.py:293
  465.4 4.7 collective-permute-start.77
  470.1 13.9 %shard_map.72 = (bf16[2,32,16,128]{3,2,1,0:T(8,128)(2,1)}, bf16[2,32,16,128]{3,2,1,0:T(8,128)(2,1)}, bf16[2,32,16,128]{3,2,1,0:T(8,128)(2,1)}, bf16[2,32,16,128]...) custom-call(bf16[2,512,512]{2,1,0:T(8,128)(2,1)} %convolution_conver, ...), custom_call_target="tpu_custom_call" | custom-call | flops 4294967296 | bytes 8388608 | tf_op jit(solution)/shard_map/pallas_call | solution.py:128
  486.2 5.6 collective-permute-done.71.refs_25_
  491.8 6.5 collective-permute-done.73.refs_27_
  498.3 6.4 collective-permute-start.54
  504.6 11.5 %collective-permute-start.56 = (bf16[2,32,16,128]{3,2,1,0:T(8,128)(2,1)}, bf16[2,32,16,128]{3,2,1,0:T(8,128)(2,1)S(1)}, u32[]{:S(2)}, u32[]{:S(2)}) collective-permute-start(bf16[2,32,16,128]{3,2,1,0:T(8,128)(2,1)} %get-tuple-element.161), channel_id=1, source_target_pairs={{0,5},{1,4},{2,7},{3,6},{4,1},{5,0},{6,3},{7,2},{8,13},{9,12},{10,... | collective-permute-start | bytes 786440 | tf_op jit(solution)/shard_map/ppermute | solution.py:293
  518.0 8.2 %collective-permute-start.60 = (bf16[2,32,16,128]{3,2,1,0:T(8,128)(2,1)}, bf16[2,32,16,128]{3,2,1,0:T(8,128)(2,1)}, u32[]{:S(2)}, u32[]{:S(2)}) collective-permute-start(bf16[2,32,16,128]{3,2,1,0:T(8,128)(2,1)} %get-tuple-element.165), channel_id=1, source_target_pairs={{0,7},{1,6},{2,5},{3,4},{4,3},{5,2},{6,1},{7,0},{8,15},{9,14},{10,... | collective-permute-start | bytes 786440 | tf_op jit(solution)/shard_map/ppermute | solution.py:293
  526.2 9.0 %collective-permute-done.54.refs_8_ = bf16[2,32,16,128]{3,2,1,0:T(8,128)(2,1)S(1)} collective-permute-done((bf16[2,32,16,128]{3,2,1,0:T(8,128)(2,1)}, bf16[2,32,16,128]{3,2,1,0:T(8,128)(2,1)S(1)}, u32[]{:S(2)}, u32[]{:S(2)}) %collective-permute-start.54) | collective-permute-done | bytes 262176 | tf_op jit(solution)/shard_map/ppermute | solution.py:293
  535.2 4.7 collective-permute-start.64
  542.9 8.3 %collective-permute-start.68 = (bf16[2,32,16,128]{3,2,1,0:T(8,128)(2,1)}, bf16[2,32,16,128]{3,2,1,0:T(8,128)(2,1)}, u32[]{:S(2)}, u32[]{:S(2)}) collective-permute-start(bf16[2,32,16,128]{3,2,1,0:T(8,128)(2,1)} %get-tuple-element.173), channel_id=1, source_target_pairs={{0,19},{1,18},{2,17},{3,16},{4,23},{5,22},{6,21},{7,20},{8,27},{9,... | collective-permute-start | bytes 786440 | tf_op jit(solution)/shard_map/ppermute | solution.py:293
  551.2 8.6 %collective-permute-start.70 = (bf16[2,32,16,128]{3,2,1,0:T(8,128)(2,1)}, bf16[2,32,16,128]{3,2,1,0:T(8,128)(2,1)}, u32[]{:S(2)}, u32[]{:S(2)}) collective-permute-start(bf16[2,32,16,128]{3,2,1,0:T(8,128)(2,1)} %get-tuple-element.175), channel_id=1, source_target_pairs={{0,20},{1,21},{2,22},{3,23},{4,16},{5,17},{6,18},{7,19},{8,28},{9,... | collective-permute-start | bytes 786440 | tf_op jit(solution)/shard_map/ppermute | solution.py:293
  559.9 3.7 collective-permute-start.74
  567.8 17.1 %collective-permute-done.70.refs_24_ = bf16[2,32,16,128]{3,2,1,0:T(8,128)(2,1)} collective-permute-done((bf16[2,32,16,128]{3,2,1,0:T(8,128)(2,1)}, bf16[2,32,16,128]{3,2,1,0:T(8,128)(2,1)}, u32[]{:S(2)}, u32[]{:S(2)}) %collective-permute-start.70) | collective-permute-done | bytes 262176 | tf_op jit(solution)/shard_map/ppermute | solution.py:293
  584.9 6.4 collective-permute-done.72.refs_26_
  591.3 14.6 %shard_map.77 = (bf16[2,128,16,128]{3,2,1,0:T(8,128)(2,1)}, bf16[2,128,16,128]{3,2,1,0:T(8,128)(2,1)}, bf16[2,128,16,128]{3,2,1,0:T(8,128)(2,1)}, bf16[2,128,16,128]{3,2,1,0:T(8,128)(2,1)}) custom-call(bf16[2,512,512]{2,1,0:T(8,128)(2,1)} %convolution_convert_fusion.6.mat_ref, bf16[2,32,16,128]{3,2,1,0:T(8,128)(2,1)} %get-tuple-element.147.refs_0_, ...), custom_call_target="tpu_custom_call" | custom-call | flops 4294967296 | bytes 8388608 | tf_op jit(solution)/shard_map/pallas_call | solution.py:128
  607.8 14.5 %shard_map.76 = (bf16[2,128,16,128]{3,2,1,0:T(8,128)(2,1)}, bf16[2,128,16,128]{3,2,1,0:T(8,128)(2,1)}, bf16[2,128,16,128]{3,2,1,0:T(8,128)(2,1)}, bf16[2,128,16,128]{3,2,1,0:T(8,128)(2,1)}) custom-call(bf16[2,512,512]{2,1,0:T(8,128)(2,1)} %convolution_convert_fusion.6.mat_ref, bf16[2,32,16,128]{3,2,1,0:T(8,128)(2,1)} %get-tuple-element.147.refs_0_, ...), custom_call_target="tpu_custom_call" | custom-call | flops 4294967296 | bytes 8388608 | tf_op jit(solution)/shard_map/pallas_call | solution.py:128
  625.2 4.5 shard_map.78.refs_0_
  632.3 21.7 %collective-permute-done.82.other_ref = bf16[2,128,16,128]{3,2,1,0:T(8,128)(2,1)} collective-permute-done((bf16[2,128,16,128]{3,2,1,0:T(8,128)(2,1)}, bf16[2,128,16,128]{3,2,1,0:T(8,128)(2,1)}, u32[]{:S(2)}, u32[]{:S(2)}) %collective-permute-start.82) | collective-permute-done | bytes 1048608 | tf_op jit(solution)/shard_map/ppermute | solution.py:283
  654.0 4.5 shard_map.79.refs_0_
  658.5 4.5 shard_map.80.refs_0_
  663.1 14.3 %collective-permute-done.78.own_ref = bf16[2,128,16,128]{3,2,1,0:T(8,128)(2,1)} collective-permute-done((bf16[2,128,16,128]{3,2,1,0:T(8,128)(2,1)}, bf16[2,128,16,128]{3,2,1,0:T(8,128)(2,1)}, u32[]{:S(2)}, u32[]{:S(2)}) %collective-permute-start.78) | collective-permute-done | bytes 1048608 | tf_op jit(solution)/shard_map/ppermute | solution.py:283
  677.3 21.4 %collective-permute-done.79.other_ref = bf16[2,128,16,128]{3,2,1,0:T(8,128)(2,1)} collective-permute-done((bf16[2,128,16,128]{3,2,1,0:T(8,128)(2,1)}, bf16[2,128,16,128]{3,2,1,0:T(8,128)(2,1)}, u32[]{:S(2)}, u32[]{:S(2)}) %collective-permute-start.79) | collective-permute-done | bytes 1048608 | tf_op jit(solution)/shard_map/ppermute | solution.py:283
  698.7 4.5 shard_map.81
  (240 shorter events, 92.6 us)
Async XLA Ops:
  20.2 27.2 %collective-permute-start.1 = (bf16[2,16,128,128]{3,2,1,0:T(8,128)(2,1)}, bf16[2,16,128,128]{3,2,1,0:T(8,128)(2,1)S(1)}, u32[]{:S(2)}, u32[]{:S(2)}) collective-permute-start(bf16[2,16,128,128]{3,2,1,0:T(8,128)(2,1)} %get-tuple-element.100), channel_id=1, source_target_pairs={{0,16},{1,17},{2,18},{3,19},{4,20},{5,21},{6,22},{7,23},{8,24},{9,... | collective-permute-start | bytes 3145736 | tf_op jit(solution)/shard_map/ppermute | solution.py:283
  23.1 45.2 %collective-permute-start.2 = (bf16[2,16,128,128]{3,2,1,0:T(8,128)(2,1)}, bf16[2,16,128,128]{3,2,1,0:T(8,128)(2,1)}, u32[]{:S(2)}, u32[]{:S(2)}) collective-permute-start(bf16[2,16,128,128]{3,2,1,0:T(8,128)(2,1)} %get-tuple-element.101), channel_id=1, source_target_pairs={{0,24},{1,25},{2,26},{3,27},{4,28},{5,29},{6,30},{7,31},{8,16},{9,... | collective-permute-start | bytes 3145736 | tf_op jit(solution)/shard_map/ppermute | solution.py:283
  33.3 35.0 %collective-permute-start = (bf16[2,16,128,128]{3,2,1,0:T(8,128)(2,1)}, bf16[2,16,128,128]{3,2,1,0:T(8,128)(2,1)}, u32[]{:S(2)}, u32[]{:S(2)}) collective-permute-start(bf16[2,16,128,128]{3,2,1,0:T(8,128)(2,1)} %get-tuple-element.99), channel_id=1, source_target_pairs={{0,8},{1,9},{2,10},{3,11},{4,12},{5,13},{6,14},{7,15},{8,0},{9,1},... | collective-permute-start | bytes 3145736 | tf_op jit(solution)/shard_map/ppermute | solution.py:283
  97.8 68.7 %collective-permute-start.3 = (bf16[2,16,128,128]{3,2,1,0:T(8,128)(2,1)}, bf16[2,16,128,128]{3,2,1,0:T(8,128)(2,1)}, u32[]{:S(2)}, u32[]{:S(2)}) collective-permute-start(bf16[2,16,128,128]{3,2,1,0:T(8,128)(2,1)} %get-tuple-element.108), channel_id=1, source_target_pairs={{0,8},{1,9},{2,10},{3,11},{4,12},{5,13},{6,14},{7,15},{8,0},{9,1},... | collective-permute-start | bytes 3145736 | tf_op jit(solution)/shard_map/ppermute | solution.py:283
  97.8 73.0 %collective-permute-start.4 = (bf16[2,16,128,128]{3,2,1,0:T(8,128)(2,1)S(1)}, bf16[2,16,128,128]{3,2,1,0:T(8,128)(2,1)}, u32[]{:S(2)}, u32[]{:S(2)}) collective-permute-start(bf16[2,16,128,128]{3,2,1,0:T(8,128)(2,1)S(1)} %copy-done.9), channel_id=1, source_target_pairs={{0,16},{1,17},{2,18},{3,19},{4,20},{5,21},{6,22},{7,23},{8,24},{9,... | collective-permute-start | bytes 3145736 | tf_op jit(solution)/shard_map/ppermute | solution.py:283
  99.2 72.0 %collective-permute-start.5 = (bf16[2,16,128,128]{3,2,1,0:T(8,128)(2,1)S(1)}, bf16[2,16,128,128]{3,2,1,0:T(8,128)(2,1)}, u32[]{:S(2)}, u32[]{:S(2)}) collective-permute-start(bf16[2,16,128,128]{3,2,1,0:T(8,128)(2,1)S(1)} %copy-done.8), channel_id=1, source_target_pairs={{0,24},{1,25},{2,26},{3,27},{4,28},{5,29},{6,30},{7,31},{8,16},{9,... | collective-permute-start | bytes 3145736 | tf_op jit(solution)/shard_map/ppermute | solution.py:283
  103.8 22.5 %collective-permute-start.14 = (bf16[2,32,16,128]{3,2,1,0:T(8,128)(2,1)}, bf16[2,32,16,128]{3,2,1,0:T(8,128)(2,1)}, u32[]{:S(2)}, u32[]{:S(2)}) collective-permute-start(bf16[2,32,16,128]{3,2,1,0:T(8,128)(2,1)} %get-tuple-element.120), channel_id=1, source_target_pairs={{0,5},{1,4},{2,7},{3,6},{4,1},{5,0},{6,3},{7,2},{8,13},{9,12},{10,... | collective-permute-start | bytes 786440 | tf_op jit(solution)/shard_map/ppermute | solution.py:293
  105.6 22.2 %collective-permute-start.16 = (bf16[2,32,16,128]{3,2,1,0:T(8,128)(2,1)}, bf16[2,32,16,128]{3,2,1,0:T(8,128)(2,1)}, u32[]{:S(2)}, u32[]{:S(2)}) collective-permute-start(bf16[2,32,16,128]{3,2,1,0:T(8,128)(2,1)} %get-tuple-element.122), channel_id=1, source_target_pairs={{0,6},{1,7},{2,4},{3,5},{4,2},{5,3},{6,0},{7,1},{8,14},{9,15},{10,... | collective-permute-start | bytes 786440 | tf_op jit(solution)/shard_map/ppermute | solution.py:293
  127.9 24.2 %collective-permute-start.20 = (bf16[2,32,16,128]{3,2,1,0:T(8,128)(2,1)}, bf16[2,32,16,128]{3,2,1,0:T(8,128)(2,1)}, u32[]{:S(2)}, u32[]{:S(2)}) collective-permute-start(bf16[2,32,16,128]{3,2,1,0:T(8,128)(2,1)} %get-tuple-element.126), channel_id=1, source_target_pairs={{0,16},{1,17},{2,18},{3,19},{4,20},{5,21},{6,22},{7,23},{8,24},{9,... | collective-permute-start | bytes 786440 | tf_op jit(solution)/shard_map/ppermute | solution.py:293
  135.8 28.0 %collective-permute-start.22 = (bf16[2,32,16,128]{3,2,1,0:T(8,128)(2,1)}, bf16[2,32,16,128]{3,2,1,0:T(8,128)(2,1)}, u32[]{:S(2)}, u32[]{:S(2)}) collective-permute-start(bf16[2,32,16,128]{3,2,1,0:T(8,128)(2,1)} %get-tuple-element.128), channel_id=1, source_target_pairs={{0,17},{1,16},{2,19},{3,18},{4,21},{5,20},{6,23},{7,22},{8,25},{9,... | collective-permute-start | bytes 786440 | tf_op jit(solution)/shard_map/ppermute | solution.py:293
  163.8 25.8 %collective-permute-start.26 = (bf16[2,32,16,128]{3,2,1,0:T(8,128)(2,1)}, bf16[2,32,16,128]{3,2,1,0:T(8,128)(2,1)}, u32[]{:S(2)}, u32[]{:S(2)}) collective-permute-start(bf16[2,32,16,128]{3,2,1,0:T(8,128)(2,1)} %get-tuple-element.132), channel_id=1, source_target_pairs={{0,19},{1,18},{2,17},{3,16},{4,23},{5,22},{6,21},{7,20},{8,27},{9,... | collective-permute-start | bytes 786440 | tf_op jit(solution)/shard_map/ppermute | solution.py:293
  166.1 34.0 %collective-permute-start.28 = (bf16[2,32,16,128]{3,2,1,0:T(8,128)(2,1)}, bf16[2,32,16,128]{3,2,1,0:T(8,128)(2,1)}, u32[]{:S(2)}, u32[]{:S(2)}) collective-permute-start(bf16[2,32,16,128]{3,2,1,0:T(8,128)(2,1)} %get-tuple-element.134), channel_id=1, source_target_pairs={{0,20},{1,21},{2,22},{3,23},{4,16},{5,17},{6,18},{7,19},{8,28},{9,... | collective-permute-start | bytes 786440 | tf_op jit(solution)/shard_map/ppermute | solution.py:293
  166.5 40.6 %collective-permute-start.30 = (bf16[2,32,16,128]{3,2,1,0:T(8,128)(2,1)}, bf16[2,32,16,128]{3,2,1,0:T(8,128)(2,1)}, u32[]{:S(2)}, u32[]{:S(2)}) collective-permute-start(bf16[2,32,16,128]{3,2,1,0:T(8,128)(2,1)} %get-tuple-element.136), channel_id=1, source_target_pairs={{0,21},{1,20},{2,23},{3,22},{4,17},{5,16},{6,19},{7,18},{8,29},{9,... | collective-permute-start | bytes 786440 | tf_op jit(solution)/shard_map/ppermute | solution.py:293
  170.9 36.3 %collective-permute-start.32 = (bf16[2,32,16,128]{3,2,1,0:T(8,128)(2,1)}, bf16[2,32,16,128]{3,2,1,0:T(8,128)(2,1)S(1)}, u32[]{:S(2)}, u32[]{:S(2)}) collective-permute-start(bf16[2,32,16,128]{3,2,1,0:T(8,128)(2,1)} %get-tuple-element.138), channel_id=1, source_target_pairs={{0,22},{1,23},{2,20},{3,21},{4,18},{5,19},{6,16},{7,17},{8,30},{9,... | collective-permute-start | bytes 786440 | tf_op jit(solution)/shard_map/ppermute | solution.py:293
  171.2 36.5 %collective-permute-start.34 = (bf16[2,32,16,128]{3,2,1,0:T(8,128)(2,1)}, bf16[2,32,16,128]{3,2,1,0:T(8,128)(2,1)S(1)}, u32[]{:S(2)}, u32[]{:S(2)}) collective-permute-start(bf16[2,32,16,128]{3,2,1,0:T(8,128)(2,1)} %get-tuple-element.140), channel_id=1, source_target_pairs={{0,23},{1,22},{2,21},{3,20},{4,19},{5,18},{6,17},{7,16},{8,31},{9,... | collective-permute-start | bytes 786440 | tf_op jit(solution)/shard_map/ppermute | solution.py:293
  189.6 21.3 %collective-permute-start.41 = (f32[6,16,64]{2,1,0:T(8,128)S(1)}, f32[6,16,64]{2,1,0:T(8,128)S(1)}, u32[]{:S(2)}, u32[]{:S(2)}) collective-permute-start(f32[6,16,64]{2,1,0:T(8,128)S(1)} %get-tuple-element.194), channel_id=1, source_target_pairs={{0,4},{1,5},{2,6},{3,7},{4,12},{5,13},{6,14},{7,15},{8,0},{9,1},{1... | collective-permute-start | bytes 73736 | tf_op jit(solution)/shard_map/ppermute | solution.py:347
  224.5 32.2 %collective-permute-start.13 = (bf16[2,32,16,128]{3,2,1,0:T(8,128)(2,1)}, bf16[2,32,16,128]{3,2,1,0:T(8,128)(2,1)}, u32[]{:S(2)}, u32[]{:S(2)}) collective-permute-start(bf16[2,32,16,128]{3,2,1,0:T(8,128)(2,1)} %get-tuple-element.119), channel_id=1, source_target_pairs={{0,4},{1,5},{2,6},{3,7},{4,0},{5,1},{6,2},{7,3},{8,12},{9,13},{10,... | collective-permute-start | bytes 786440 | tf_op jit(solution)/shard_map/ppermute | solution.py:293
  227.0 36.2 %collective-permute-start.15 = (bf16[2,32,16,128]{3,2,1,0:T(8,128)(2,1)}, bf16[2,32,16,128]{3,2,1,0:T(8,128)(2,1)}, u32[]{:S(2)}, u32[]{:S(2)}) collective-permute-start(bf16[2,32,16,128]{3,2,1,0:T(8,128)(2,1)} %get-tuple-element.121), channel_id=1, source_target_pairs={{0,5},{1,4},{2,7},{3,6},{4,1},{5,0},{6,3},{7,2},{8,13},{9,12},{10,... | collective-permute-start | bytes 786440 | tf_op jit(solution)/shard_map/ppermute | solution.py:293
  228.5 34.7 %collective-permute-start.17 = (bf16[2,32,16,128]{3,2,1,0:T(8,128)(2,1)}, bf16[2,32,16,128]{3,2,1,0:T(8,128)(2,1)S(1)}, u32[]{:S(2)}, u32[]{:S(2)}) collective-permute-start(bf16[2,32,16,128]{3,2,1,0:T(8,128)(2,1)} %get-tuple-element.123), channel_id=1, source_target_pairs={{0,6},{1,7},{2,4},{3,5},{4,2},{5,3},{6,0},{7,1},{8,14},{9,15},{10,... | collective-permute-start | bytes 786440 | tf_op jit(solution)/shard_map/ppermute | solution.py:293
  231.6 36.5 %collective-permute-start.19 = (bf16[2,32,16,128]{3,2,1,0:T(8,128)(2,1)}, bf16[2,32,16,128]{3,2,1,0:T(8,128)(2,1)S(1)}, u32[]{:S(2)}, u32[]{:S(2)}) collective-permute-start(bf16[2,32,16,128]{3,2,1,0:T(8,128)(2,1)} %get-tuple-element.125), channel_id=1, source_target_pairs={{0,7},{1,6},{2,5},{3,4},{4,3},{5,2},{6,1},{7,0},{8,15},{9,14},{10,... | collective-permute-start | bytes 786440 | tf_op jit(solution)/shard_map/ppermute | solution.py:293
  242.6 32.1 %collective-permute-start.21 = (bf16[2,32,16,128]{3,2,1,0:T(8,128)(2,1)}, bf16[2,32,16,128]{3,2,1,0:T(8,128)(2,1)S(1)}, u32[]{:S(2)}, u32[]{:S(2)}) collective-permute-start(bf16[2,32,16,128]{3,2,1,0:T(8,128)(2,1)} %get-tuple-element.127), channel_id=1, source_target_pairs={{0,16},{1,17},{2,18},{3,19},{4,20},{5,21},{6,22},{7,23},{8,24},{9,... | collective-permute-start | bytes 786440 | tf_op jit(solution)/shard_map/ppermute | solution.py:293
  263.2 26.4 %collective-permute-start.27 = (bf16[2,32,16,128]{3,2,1,0:T(8,128)(2,1)}, bf16[2,32,16,128]{3,2,1,0:T(8,128)(2,1)S(1)}, u32[]{:S(2)}, u32[]{:S(2)}) collective-permute-start(bf16[2,32,16,128]{3,2,1,0:T(8,128)(2,1)} %get-tuple-element.133), channel_id=1, source_target_pairs={{0,19},{1,18},{2,17},{3,16},{4,23},{5,22},{6,21},{7,20},{8,27},{9,... | collective-permute-start | bytes 786440 | tf_op jit(solution)/shard_map/ppermute | solution.py:293
  268.1 36.9 %collective-permute-start.29 = (bf16[2,32,16,128]{3,2,1,0:T(8,128)(2,1)}, bf16[2,32,16,128]{3,2,1,0:T(8,128)(2,1)S(1)}, u32[]{:S(2)}, u32[]{:S(2)}) collective-permute-start(bf16[2,32,16,128]{3,2,1,0:T(8,128)(2,1)} %get-tuple-element.135), channel_id=1, source_target_pairs={{0,20},{1,21},{2,22},{3,23},{4,16},{5,17},{6,18},{7,19},{8,28},{9,... | collective-permute-start | bytes 786440 | tf_op jit(solution)/shard_map/ppermute | solution.py:293
  274.7 37.8 %collective-permute-start.31 = (bf16[2,32,16,128]{3,2,1,0:T(8,128)(2,1)}, bf16[2,32,16,128]{3,2,1,0:T(8,128)(2,1)S(1)}, u32[]{:S(2)}, u32[]{:S(2)}) collective-permute-start(bf16[2,32,16,128]{3,2,1,0:T(8,128)(2,1)} %get-tuple-element.137), channel_id=1, source_target_pairs={{0,21},{1,20},{2,23},{3,22},{4,17},{5,16},{6,19},{7,18},{8,29},{9,... | collective-permute-start | bytes 786440 | tf_op jit(solution)/shard_map/ppermute | solution.py:293
  276.7 36.0 %collective-permute-start.33 = (bf16[2,32,16,128]{3,2,1,0:T(8,128)(2,1)S(1)}, bf16[2,32,16,128]{3,2,1,0:T(8,128)(2,1)S(1)}, u32[]{:S(2)}, u32[]{:S(2)}) collective-permute-start(bf16[2,32,16,128]{3,2,1,0:T(8,128)(2,1)S(1)} %copy-done.14), channel_id=1, source_target_pairs={{0,22},{1,23},{2,20},{3,21},{4,18},{5,19},{6,16},{7,17},{8,30},{9,... | collective-permute-start | bytes 786440 | tf_op jit(solution)/shard_map/ppermute | solution.py:293
  278.8 34.0 %collective-permute-start.35 = (bf16[2,32,16,128]{3,2,1,0:T(8,128)(2,1)S(1)}, bf16[2,32,16,128]{3,2,1,0:T(8,128)(2,1)S(1)}, u32[]{:S(2)}, u32[]{:S(2)}) collective-permute-start(bf16[2,32,16,128]{3,2,1,0:T(8,128)(2,1)S(1)} %copy-done.13), channel_id=1, source_target_pairs={{0,23},{1,22},{2,21},{3,20},{4,19},{5,18},{6,17},{7,16},{8,31},{9,... | collective-permute-start | bytes 786440 | tf_op jit(solution)/shard_map/ppermute | solution.py:293
  289.7 45.7 %collective-permute-start.44 = (f32[6,16,64]{2,1,0:T(8,128)S(1)}, f32[6,16,64]{2,1,0:T(8,128)S(1)}, u32[]{:S(2)}, u32[]{:S(2)}) collective-permute-start(f32[6,16,64]{2,1,0:T(8,128)S(1)} %get-tuple-element.191), channel_id=1, source_target_pairs={{0,7},{1,6},{2,5},{3,4},{4,15},{5,14},{6,13},{7,12},{8,3},{9,2},{1... | collective-permute-start | bytes 73736 | tf_op jit(solution)/shard_map/ppermute | solution.py:347
  305.1 30.3 %collective-permute-start.43 = (f32[6,16,64]{2,1,0:T(8,128)S(1)}, f32[6,16,64]{2,1,0:T(8,128)S(1)}, u32[]{:S(2)}, u32[]{:S(2)}) collective-permute-start(f32[6,16,64]{2,1,0:T(8,128)S(1)} %get-tuple-element.192), channel_id=1, source_target_pairs={{0,6},{1,7},{2,4},{3,5},{4,14},{5,15},{6,12},{7,13},{8,2},{9,3},{1... | collective-permute-start | bytes 73736 | tf_op jit(solution)/shard_map/ppermute | solution.py:347
  324.1 20.9 %collective-permute-start.46 = (bf16[2,16,256,128]{3,2,1,0:T(8,128)(2,1)}, bf16[2,16,256,128]{3,2,1,0:T(8,128)(2,1)}, u32[]{:S(2)}, u32[]{:S(2)}) collective-permute-start(bf16[2,16,256,128]{3,2,1,0:T(8,128)(2,1)} %get-tuple-element.149), channel_id=1, source_target_pairs={{0,8},{1,9},{2,10},{3,11},{4,12},{5,13},{6,14},{7,15},{8,0},{9,1},... | collective-permute-start | bytes 6291464 | tf_op jit(solution)/shard_map/ppermute | solution.py:283
  334.8 26.0 %collective-permute-start.36 = (bf16[2,16,256,128]{3,2,1,0:T(8,128)(2,1)}, bf16[2,16,256,128]{3,2,1,0:T(8,128)(2,1)S(1)}, u32[]{:S(2)}, u32[]{:S(2)}) collective-permute-start(bf16[2,16,256,128]{3,2,1,0:T(8,128)(2,1)} %get-tuple-element.143), channel_id=1, source_target_pairs={{0,8},{1,9},{2,10},{3,11},{4,12},{5,13},{6,14},{7,15},{8,0},{9,1},... | collective-permute-start | bytes 6291464 | tf_op jit(solution)/shard_map/ppermute | solution.py:283
  377.8 31.8 %collective-permute-start.45 = (bf16[2,16,256,128]{3,2,1,0:T(8,128)(2,1)}, bf16[2,16,256,128]{3,2,1,0:T(8,128)(2,1)}, u32[]{:S(2)}, u32[]{:S(2)}) collective-permute-start(bf16[2,16,256,128]{3,2,1,0:T(8,128)(2,1)} %get-tuple-element.146), channel_id=1, source_target_pairs={{0,8},{1,9},{2,10},{3,11},{4,12},{5,13},{6,14},{7,15},{8,0},{9,1},... | collective-permute-start | bytes 6291464 | tf_op jit(solution)/shard_map/ppermute | solution.py:283
  395.7 28.0 %collective-permute-start.51 = (bf16[2,32,16,128]{3,2,1,0:T(8,128)(2,1)}, bf16[2,32,16,128]{3,2,1,0:T(8,128)(2,1)S(1)}, u32[]{:S(2)}, u32[]{:S(2)}) collective-permute-start(bf16[2,32,16,128]{3,2,1,0:T(8,128)(2,1)} %get-tuple-element.156), channel_id=1, source_target_pairs={{0,2},{1,3},{2,0},{3,1},{4,6},{5,7},{6,4},{7,5},{8,10},{9,11},{10,... | collective-permute-start | bytes 786440 | tf_op jit(solution)/shard_map/ppermute | solution.py:293
  406.5 23.0 %collective-permute-start.53 = (bf16[2,32,16,128]{3,2,1,0:T(8,128)(2,1)}, bf16[2,32,16,128]{3,2,1,0:T(8,128)(2,1)S(1)}, u32[]{:S(2)}, u32[]{:S(2)}) collective-permute-start(bf16[2,32,16,128]{3,2,1,0:T(8,128)(2,1)} %get-tuple-element.158), channel_id=1, source_target_pairs={{0,3},{1,2},{2,1},{3,0},{4,7},{5,6},{6,5},{7,4},{8,11},{9,10},{10,... | collective-permute-start | bytes 786440 | tf_op jit(solution)/shard_map/ppermute | solution.py:293
  407.2 24.2 %collective-permute-start.55 = (bf16[2,32,16,128]{3,2,1,0:T(8,128)(2,1)}, bf16[2,32,16,128]{3,2,1,0:T(8,128)(2,1)S(1)}, u32[]{:S(2)}, u32[]{:S(2)}) collective-permute-start(bf16[2,32,16,128]{3,2,1,0:T(8,128)(2,1)} %get-tuple-element.160), channel_id=1, source_target_pairs={{0,4},{1,5},{2,6},{3,7},{4,0},{5,1},{6,2},{7,3},{8,12},{9,13},{10,... | collective-permute-start | bytes 786440 | tf_op jit(solution)/shard_map/ppermute | solution.py:293
  409.6 38.8 %collective-permute-start.57 = (bf16[2,32,16,128]{3,2,1,0:T(8,128)(2,1)}, bf16[2,32,16,128]{3,2,1,0:T(8,128)(2,1)S(1)}, u32[]{:S(2)}, u32[]{:S(2)}) collective-permute-start(bf16[2,32,16,128]{3,2,1,0:T(8,128)(2,1)} %get-tuple-element.162), channel_id=1, source_target_pairs={{0,5},{1,4},{2,7},{3,6},{4,1},{5,0},{6,3},{7,2},{8,13},{9,12},{10,... | collective-permute-start | bytes 786440 | tf_op jit(solution)/shard_map/ppermute | solution.py:293
  410.3 38.6 %collective-permute-start.59 = (bf16[2,32,16,128]{3,2,1,0:T(8,128)(2,1)}, bf16[2,32,16,128]{3,2,1,0:T(8,128)(2,1)S(1)}, u32[]{:S(2)}, u32[]{:S(2)}) collective-permute-start(bf16[2,32,16,128]{3,2,1,0:T(8,128)(2,1)} %get-tuple-element.164), channel_id=1, source_target_pairs={{0,6},{1,7},{2,4},{3,5},{4,2},{5,3},{6,0},{7,1},{8,14},{9,15},{10,... | collective-permute-start | bytes 786440 | tf_op jit(solution)/shard_map/ppermute | solution.py:293
  423.7 31.6 %collective-permute-start.61 = (bf16[2,32,16,128]{3,2,1,0:T(8,128)(2,1)}, bf16[2,32,16,128]{3,2,1,0:T(8,128)(2,1)S(1)}, u32[]{:S(2)}, u32[]{:S(2)}) collective-permute-start(bf16[2,32,16,128]{3,2,1,0:T(8,128)(2,1)} %get-tuple-element.166), channel_id=1, source_target_pairs={{0,7},{1,6},{2,5},{3,4},{4,3},{5,2},{6,1},{7,0},{8,15},{9,14},{10,... | collective-permute-start | bytes 786440 | tf_op jit(solution)/shard_map/ppermute | solution.py:293
  429.5 33.5 %collective-permute-start.63 = (bf16[2,32,16,128]{3,2,1,0:T(8,128)(2,1)}, bf16[2,32,16,128]{3,2,1,0:T(8,128)(2,1)S(1)}, u32[]{:S(2)}, u32[]{:S(2)}) collective-permute-start(bf16[2,32,16,128]{3,2,1,0:T(8,128)(2,1)} %get-tuple-element.168), channel_id=1, source_target_pairs={{0,16},{1,17},{2,18},{3,19},{4,20},{5,21},{6,22},{7,23},{8,24},{9,... | collective-permute-start | bytes 786440 | tf_op jit(solution)/shard_map/ppermute | solution.py:293
  431.3 34.0 %collective-permute-start.65 = (bf16[2,32,16,128]{3,2,1,0:T(8,128)(2,1)}, bf16[2,32,16,128]{3,2,1,0:T(8,128)(2,1)S(1)}, u32[]{:S(2)}, u32[]{:S(2)}) collective-permute-start(bf16[2,32,16,128]{3,2,1,0:T(8,128)(2,1)} %get-tuple-element.170), channel_id=1, source_target_pairs={{0,17},{1,16},{2,19},{3,18},{4,21},{5,20},{6,23},{7,22},{8,25},{9,... | collective-permute-start | bytes 786440 | tf_op jit(solution)/shard_map/ppermute | solution.py:293
  448.9 35.1 %collective-permute-start.69 = (bf16[2,32,16,128]{3,2,1,0:T(8,128)(2,1)}, bf16[2,32,16,128]{3,2,1,0:T(8,128)(2,1)S(1)}, u32[]{:S(2)}, u32[]{:S(2)}) collective-permute-start(bf16[2,32,16,128]{3,2,1,0:T(8,128)(2,1)} %get-tuple-element.174), channel_id=1, source_target_pairs={{0,19},{1,18},{2,17},{3,16},{4,23},{5,22},{6,21},{7,20},{8,27},{9,... | collective-permute-start | bytes 786440 | tf_op jit(solution)/shard_map/ppermute | solution.py:293
  455.3 36.5 %collective-permute-start.71 = (bf16[2,32,16,128]{3,2,1,0:T(8,128)(2,1)}, bf16[2,32,16,128]{3,2,1,0:T(8,128)(2,1)}, u32[]{:S(2)}, u32[]{:S(2)}) collective-permute-start(bf16[2,32,16,128]{3,2,1,0:T(8,128)(2,1)} %get-tuple-element.176), channel_id=1, source_target_pairs={{0,20},{1,21},{2,22},{3,23},{4,16},{5,17},{6,18},{7,19},{8,28},{9,... | collective-permute-start | bytes 786440 | tf_op jit(solution)/shard_map/ppermute | solution.py:293
  463.0 35.2 %collective-permute-start.73 = (bf16[2,32,16,128]{3,2,1,0:T(8,128)(2,1)}, bf16[2,32,16,128]{3,2,1,0:T(8,128)(2,1)}, u32[]{:S(2)}, u32[]{:S(2)}) collective-permute-start(bf16[2,32,16,128]{3,2,1,0:T(8,128)(2,1)} %get-tuple-element.178), channel_id=1, source_target_pairs={{0,21},{1,20},{2,23},{3,22},{4,17},{5,16},{6,19},{7,18},{8,29},{9,... | collective-permute-start | bytes 786440 | tf_op jit(solution)/shard_map/ppermute | solution.py:293
  465.3 32.9 %collective-permute-start.75 = (bf16[2,32,16,128]{3,2,1,0:T(8,128)(2,1)}, bf16[2,32,16,128]{3,2,1,0:T(8,128)(2,1)}, u32[]{:S(2)}, u32[]{:S(2)}) collective-permute-start(bf16[2,32,16,128]{3,2,1,0:T(8,128)(2,1)} %get-tuple-element.180), channel_id=1, source_target_pairs={{0,22},{1,23},{2,20},{3,21},{4,18},{5,19},{6,16},{7,17},{8,30},{9,... | collective-permute-start | bytes 786440 | tf_op jit(solution)/shard_map/ppermute | solution.py:293
  465.4 39.3 %collective-permute-start.77 = (bf16[2,32,16,128]{3,2,1,0:T(8,128)(2,1)}, bf16[2,32,16,128]{3,2,1,0:T(8,128)(2,1)}, u32[]{:S(2)}, u32[]{:S(2)}) collective-permute-start(bf16[2,32,16,128]{3,2,1,0:T(8,128)(2,1)} %get-tuple-element.182), channel_id=1, source_target_pairs={{0,23},{1,22},{2,21},{3,20},{4,19},{5,18},{6,17},{7,16},{8,31},{9,... | collective-permute-start | bytes 786440 | tf_op jit(solution)/shard_map/ppermute | solution.py:293
  484.7 31.4 %collective-permute-start.48 = (bf16[2,32,16,128]{3,2,1,0:T(8,128)(2,1)}, bf16[2,32,16,128]{3,2,1,0:T(8,128)(2,1)S(1)}, u32[]{:S(2)}, u32[]{:S(2)}) collective-permute-start(bf16[2,32,16,128]{3,2,1,0:T(8,128)(2,1)} %get-tuple-element.153), channel_id=1, source_target_pairs={{0,1},{1,0},{2,3},{3,2},{4,5},{5,4},{6,7},{7,6},{8,9},{9,8},{10,11... | collective-permute-start | bytes 786440 | tf_op jit(solution)/shard_map/ppermute | solution.py:293
  491.8 26.2 %collective-permute-start.50 = (bf16[2,32,16,128]{3,2,1,0:T(8,128)(2,1)}, bf16[2,32,16,128]{3,2,1,0:T(8,128)(2,1)S(1)}, u32[]{:S(2)}, u32[]{:S(2)}) collective-permute-start(bf16[2,32,16,128]{3,2,1,0:T(8,128)(2,1)} %get-tuple-element.155), channel_id=1, source_target_pairs={{0,2},{1,3},{2,0},{3,1},{4,6},{5,7},{6,4},{7,5},{8,10},{9,11},{10,... | collective-permute-start | bytes 786440 | tf_op jit(solution)/shard_map/ppermute | solution.py:293
  498.3 27.9 %collective-permute-start.52 = (bf16[2,32,16,128]{3,2,1,0:T(8,128)(2,1)}, bf16[2,32,16,128]{3,2,1,0:T(8,128)(2,1)S(1)}, u32[]{:S(2)}, u32[]{:S(2)}) collective-permute-start(bf16[2,32,16,128]{3,2,1,0:T(8,128)(2,1)} %get-tuple-element.157), channel_id=1, source_target_pairs={{0,3},{1,2},{2,1},{3,0},{4,7},{5,6},{6,5},{7,4},{8,11},{9,10},{10,... | collective-permute-start | bytes 786440 | tf_op jit(solution)/shard_map/ppermute | solution.py:293
  498.3 36.9 %collective-permute-start.54 = (bf16[2,32,16,128]{3,2,1,0:T(8,128)(2,1)}, bf16[2,32,16,128]{3,2,1,0:T(8,128)(2,1)S(1)}, u32[]{:S(2)}, u32[]{:S(2)}) collective-permute-start(bf16[2,32,16,128]{3,2,1,0:T(8,128)(2,1)} %get-tuple-element.159), channel_id=1, source_target_pairs={{0,4},{1,5},{2,6},{3,7},{4,0},{5,1},{6,2},{7,3},{8,12},{9,13},{10,... | collective-permute-start | bytes 786440 | tf_op jit(solution)/shard_map/ppermute | solution.py:293
  504.6 38.2 %collective-permute-start.56 = (bf16[2,32,16,128]{3,2,1,0:T(8,128)(2,1)}, bf16[2,32,16,128]{3,2,1,0:T(8,128)(2,1)S(1)}, u32[]{:S(2)}, u32[]{:S(2)}) collective-permute-start(bf16[2,32,16,128]{3,2,1,0:T(8,128)(2,1)} %get-tuple-element.161), channel_id=1, source_target_pairs={{0,5},{1,4},{2,7},{3,6},{4,1},{5,0},{6,3},{7,2},{8,13},{9,12},{10,... | collective-permute-start | bytes 786440 | tf_op jit(solution)/shard_map/ppermute | solution.py:293
  516.1 26.8 %collective-permute-start.58 = (bf16[2,32,16,128]{3,2,1,0:T(8,128)(2,1)}, bf16[2,32,16,128]{3,2,1,0:T(8,128)(2,1)}, u32[]{:S(2)}, u32[]{:S(2)}) collective-permute-start(bf16[2,32,16,128]{3,2,1,0:T(8,128)(2,1)} %get-tuple-element.163), channel_id=1, source_target_pairs={{0,6},{1,7},{2,4},{3,5},{4,2},{5,3},{6,0},{7,1},{8,14},{9,15},{10,... | collective-permute-start | bytes 786440 | tf_op jit(solution)/shard_map/ppermute | solution.py:293
  518.0 33.2 %collective-permute-start.60 = (bf16[2,32,16,128]{3,2,1,0:T(8,128)(2,1)}, bf16[2,32,16,128]{3,2,1,0:T(8,128)(2,1)}, u32[]{:S(2)}, u32[]{:S(2)}) collective-permute-start(bf16[2,32,16,128]{3,2,1,0:T(8,128)(2,1)} %get-tuple-element.165), channel_id=1, source_target_pairs={{0,7},{1,6},{2,5},{3,4},{4,3},{5,2},{6,1},{7,0},{8,15},{9,14},{10,... | collective-permute-start | bytes 786440 | tf_op jit(solution)/shard_map/ppermute | solution.py:293
  526.2 33.6 %collective-permute-start.62 = (bf16[2,32,16,128]{3,2,1,0:T(8,128)(2,1)}, bf16[2,32,16,128]{3,2,1,0:T(8,128)(2,1)}, u32[]{:S(2)}, u32[]{:S(2)}) collective-permute-start(bf16[2,32,16,128]{3,2,1,0:T(8,128)(2,1)} %get-tuple-element.167), channel_id=1, source_target_pairs={{0,16},{1,17},{2,18},{3,19},{4,20},{5,21},{6,22},{7,23},{8,24},{9,... | collective-permute-start | bytes 786440 | tf_op jit(solution)/shard_map/ppermute | solution.py:293
  535.2 24.7 %collective-permute-start.64 = (bf16[2,32,16,128]{3,2,1,0:T(8,128)(2,1)}, bf16[2,32,16,128]{3,2,1,0:T(8,128)(2,1)}, u32[]{:S(2)}, u32[]{:S(2)}) collective-permute-start(bf16[2,32,16,128]{3,2,1,0:T(8,128)(2,1)} %get-tuple-element.169), channel_id=1, source_target_pairs={{0,17},{1,16},{2,19},{3,18},{4,21},{5,20},{6,23},{7,22},{8,25},{9,... | collective-permute-start | bytes 786440 | tf_op jit(solution)/shard_map/ppermute | solution.py:293
  542.9 20.7 %collective-permute-start.66 = (bf16[2,32,16,128]{3,2,1,0:T(8,128)(2,1)}, bf16[2,32,16,128]{3,2,1,0:T(8,128)(2,1)}, u32[]{:S(2)}, u32[]{:S(2)}) collective-permute-start(bf16[2,32,16,128]{3,2,1,0:T(8,128)(2,1)} %get-tuple-element.171), channel_id=1, source_target_pairs={{0,18},{1,19},{2,16},{3,17},{4,22},{5,23},{6,20},{7,21},{8,26},{9,... | collective-permute-start | bytes 786440 | tf_op jit(solution)/shard_map/ppermute | solution.py:293
  542.9 24.9 %collective-permute-start.68 = (bf16[2,32,16,128]{3,2,1,0:T(8,128)(2,1)}, bf16[2,32,16,128]{3,2,1,0:T(8,128)(2,1)}, u32[]{:S(2)}, u32[]{:S(2)}) collective-permute-start(bf16[2,32,16,128]{3,2,1,0:T(8,128)(2,1)} %get-tuple-element.173), channel_id=1, source_target_pairs={{0,19},{1,18},{2,17},{3,16},{4,23},{5,22},{6,21},{7,20},{8,27},{9,... | collective-permute-start | bytes 786440 | tf_op jit(solution)/shard_map/ppermute | solution.py:293
  551.2 33.7 %collective-permute-start.70 = (bf16[2,32,16,128]{3,2,1,0:T(8,128)(2,1)}, bf16[2,32,16,128]{3,2,1,0:T(8,128)(2,1)}, u32[]{:S(2)}, u32[]{:S(2)}) collective-permute-start(bf16[2,32,16,128]{3,2,1,0:T(8,128)(2,1)} %get-tuple-element.175), channel_id=1, source_target_pairs={{0,20},{1,21},{2,22},{3,23},{4,16},{5,17},{6,18},{7,19},{8,28},{9,... | collective-permute-start | bytes 786440 | tf_op jit(solution)/shard_map/ppermute | solution.py:293
  559.8 31.4 %collective-permute-start.72 = (bf16[2,32,16,128]{3,2,1,0:T(8,128)(2,1)}, bf16[2,32,16,128]{3,2,1,0:T(8,128)(2,1)}, u32[]{:S(2)}, u32[]{:S(2)}) collective-permute-start(bf16[2,32,16,128]{3,2,1,0:T(8,128)(2,1)} %get-tuple-element.177), channel_id=1, source_target_pairs={{0,21},{1,20},{2,23},{3,22},{4,17},{5,16},{6,19},{7,18},{8,29},{9,... | collective-permute-start | bytes 786440 | tf_op jit(solution)/shard_map/ppermute | solution.py:293
  559.9 31.4 %collective-permute-start.74 = (bf16[2,32,16,128]{3,2,1,0:T(8,128)(2,1)}, bf16[2,32,16,128]{3,2,1,0:T(8,128)(2,1)}, u32[]{:S(2)}, u32[]{:S(2)}) collective-permute-start(bf16[2,32,16,128]{3,2,1,0:T(8,128)(2,1)} %get-tuple-element.179), channel_id=1, source_target_pairs={{0,22},{1,23},{2,20},{3,21},{4,18},{5,19},{6,16},{7,17},{8,30},{9,... | collective-permute-start | bytes 786440 | tf_op jit(solution)/shard_map/ppermute | solution.py:293
  563.6 27.7 %collective-permute-start.76 = (bf16[2,32,16,128]{3,2,1,0:T(8,128)(2,1)}, bf16[2,32,16,128]{3,2,1,0:T(8,128)(2,1)}, u32[]{:S(2)}, u32[]{:S(2)}) collective-permute-start(bf16[2,32,16,128]{3,2,1,0:T(8,128)(2,1)} %get-tuple-element.181), channel_id=1, source_target_pairs={{0,23},{1,22},{2,21},{3,20},{4,19},{5,18},{6,17},{7,16},{8,31},{9,... | collective-permute-start | bytes 786440 | tf_op jit(solution)/shard_map/ppermute | solution.py:293
  606.0 26.3 %collective-permute-start.81 = (bf16[2,128,16,128]{3,2,1,0:T(8,128)(2,1)}, bf16[2,128,16,128]{3,2,1,0:T(8,128)(2,1)S(1)}, u32[]{:S(2)}, u32[]{:S(2)}) collective-permute-start(bf16[2,128,16,128]{3,2,1,0:T(8,128)(2,1)} %get-tuple-element.187), channel_id=1, source_target_pairs={{0,16},{1,17},{2,18},{3,19},{4,20},{5,21},{6,22},{7,23},{8,24},{9,... | collective-permute-start | bytes 3145736 | tf_op jit(solution)/shard_map/ppermute | solution.py:283
  607.6 46.3 %collective-permute-start.82 = (bf16[2,128,16,128]{3,2,1,0:T(8,128)(2,1)}, bf16[2,128,16,128]{3,2,1,0:T(8,128)(2,1)}, u32[]{:S(2)}, u32[]{:S(2)}) collective-permute-start(bf16[2,128,16,128]{3,2,1,0:T(8,128)(2,1)} %get-tuple-element.188), channel_id=1, source_target_pairs={{0,24},{1,25},{2,26},{3,27},{4,28},{5,29},{6,30},{7,31},{8,16},{9,... | collective-permute-start | bytes 3145736 | tf_op jit(solution)/shard_map/ppermute | solution.py:283
  622.3 36.2 %collective-permute-start.80 = (bf16[2,128,16,128]{3,2,1,0:T(8,128)(2,1)}, bf16[2,128,16,128]{3,2,1,0:T(8,128)(2,1)}, u32[]{:S(2)}, u32[]{:S(2)}) collective-permute-start(bf16[2,128,16,128]{3,2,1,0:T(8,128)(2,1)} %get-tuple-element.186), channel_id=1, source_target_pairs={{0,8},{1,9},{2,10},{3,11},{4,12},{5,13},{6,14},{7,15},{8,0},{9,1},... | collective-permute-start | bytes 3145736 | tf_op jit(solution)/shard_map/ppermute | solution.py:283
  622.7 54.6 %collective-permute-start.78 = (bf16[2,128,16,128]{3,2,1,0:T(8,128)(2,1)}, bf16[2,128,16,128]{3,2,1,0:T(8,128)(2,1)}, u32[]{:S(2)}, u32[]{:S(2)}) collective-permute-start(bf16[2,128,16,128]{3,2,1,0:T(8,128)(2,1)} %get-tuple-element.183), channel_id=1, source_target_pairs={{0,16},{1,17},{2,18},{3,19},{4,20},{5,21},{6,22},{7,23},{8,24},{9,... | collective-permute-start | bytes 3145736 | tf_op jit(solution)/shard_map/ppermute | solution.py:283
  624.3 74.4 %collective-permute-start.79 = (bf16[2,128,16,128]{3,2,1,0:T(8,128)(2,1)}, bf16[2,128,16,128]{3,2,1,0:T(8,128)(2,1)}, u32[]{:S(2)}, u32[]{:S(2)}) collective-permute-start(bf16[2,128,16,128]{3,2,1,0:T(8,128)(2,1)} %get-tuple-element.184), channel_id=1, source_target_pairs={{0,24},{1,25},{2,26},{3,27},{4,28},{5,29},{6,30},{7,31},{8,16},{9,... | collective-permute-start | bytes 3145736 | tf_op jit(solution)/shard_map/ppermute | solution.py:283
  (63 other events, 1808.4 us)
